TPU v7x, 32 devices: a whole 2x2x4 slice. The times are simulated.
32 devices in a mesh: grp: 4 (over x, core), sub: 8 (over z, y).
Axes of the slice: x: 2, y: 2, z: 4, core: 2. Of those that a mesh axis runs over, the one named last changes fastest.
Arguments:
- shell_state: float32 [2, 48, 262144], P(None, None, ('grp', 'sub')), may hold values from -6 to 6
- source: bfloat16 [2, 256, 16, 768], P(None, ('grp', 'sub')), may hold values from -6 to 6
- knockdown: bfloat16 [256, 16, 768], P(('grp', 'sub')), may hold values from 0.29882812 to 3
- orient: int32 [256, 48], P(('grp', 'sub')), may hold values from 0 to 3
- active: int32 [256], P(('grp', 'sub')), may hold values from 24 to 48
- point_owner: int32 [256, 64], P(('grp', 'sub')), may hold values from 0 to 31, as said below
- owner_nodes: int32 [32, 32, 32], P(('grp', 'sub')), may hold values from -1 to 8191, as said below
Outputs:
- adjoint: float32 [2, 256, 16, 768], P(None, ('grp', 'sub'))
- shell_force: float32 [2, 48, 262144], P(None, None, ('grp', 'sub'))
Inputs may be any that keep to these rules, and one draw needn't show every extreme that they name: `point_owner`: within every block of boundary columns (see the steps), no owner appears more than 32 times, and in every draw one owner, the same for all blocks, appears exactly 32 times in each block. owner_nodes[o, d, r] is the local node of the column of block d with owner o that has r earlier such columns, and -1 for r at or beyond the count of such columns.
All inputs are finite; a program needn't handle non-finite values.
Results may differ from a plain program's by a relative error of at most 0.0003.
Values sent between devices are 32-bit elements; how exact they have to be, the bound alone decides.
No kernel may reach another device: no remote copies, remote signals or barrier semaphores. Data moves between devices by JAX's collectives and lax.ppermute only.
A program may use at most 64 MiB of HBM per device.

v0:
```python
import math

import jax
import jax.numpy as jnp
from jax import lax
from jax.sharding import PartitionSpec as P

SWEEPS = 3
STEPS = 2


FIBER_COND = 1.0
TRANSVERSE = 0.25
THROUGH = 0.15
MASS_SHARE = 0.05
CHEB_CENTER = 1.02
CHEB_HALF = 0.98


def face_mean(lower_side, upper_side):
    return jnp.where((lower_side > 0) & (upper_side > 0), 0.5 * (lower_side + upper_side), 0.0)


def flat_coeffs(knock_flat, orient, active, side_cells):
    sub_count, side_x, flat_width = knock_flat.shape
    ply_count = orient.shape[1]
    active_mask = (jnp.arange(ply_count)[None, :] < active[:, None]).astype(jnp.float32)
    ply_angle = orient.astype(jnp.float32) * (math.pi / 6.0)
    cos_square = jnp.cos(ply_angle) ** 2
    fiber_part = (FIBER_COND * cos_square + TRANSVERSE * (1.0 - cos_square)) * active_mask
    cross_part = (FIBER_COND * (1.0 - cos_square) + TRANSVERSE * cos_square) * active_mask
    fiber_flat = jnp.repeat(fiber_part, side_cells, axis=1)[:, None, :]
    cross_flat = jnp.repeat(cross_part, side_cells, axis=1)[:, None, :]
    mask_flat = jnp.repeat(active_mask, side_cells, axis=1)[:, None, :]
    along_x = knock_flat * fiber_flat
    along_y = knock_flat * cross_flat
    across_ply = knock_flat * (THROUGH * mask_flat)
    flat_place = jnp.arange(flat_width)
    y_place = (flat_place % side_cells)[None, None, :]
    ply_place = (flat_place // side_cells)[None, None, :]
    x_place = jnp.arange(side_x)[None, :, None]
    face_west = jnp.where(x_place == 0, 0.0, face_mean(jnp.roll(along_x, 1, axis=1), along_x))
    face_east = jnp.where(
        x_place == side_x - 1, 0.0, face_mean(along_x, jnp.roll(along_x, -1, axis=1))
    )
    face_south = jnp.where(y_place == 0, 0.0, face_mean(jnp.roll(along_y, 1, axis=2), along_y))
    face_north = jnp.where(
        y_place == side_cells - 1, 0.0, face_mean(along_y, jnp.roll(along_y, -1, axis=2))
    )
    face_below = jnp.where(
        ply_place == 0, 0.0, face_mean(jnp.roll(across_ply, side_cells, axis=2), across_ply)
    )
    face_above = jnp.where(
        ply_place == ply_count - 1,
        0.0,
        face_mean(across_ply, jnp.roll(across_ply, -side_cells, axis=2)),
    )
    ghost_west = jnp.where(x_place == 0, along_x, 0.0)
    ghost_east = jnp.where(x_place == side_x - 1, along_x, 0.0)
    ghost_south = jnp.where(y_place == 0, along_y, 0.0)
    ghost_north = jnp.where(y_place == side_cells - 1, along_y, 0.0)
    diagonal = (
        face_west
        + face_east
        + face_south
        + face_north
        + face_below
        + face_above
        + ghost_west
        + ghost_east
        + ghost_south
        + ghost_north
        + MASS_SHARE * (along_x + along_y + across_ply)
        + (1.0 - mask_flat)
    )
    return (
        face_west,
        face_east,
        face_south,
        face_north,
        face_below,
        face_above,
        ghost_west,
        ghost_east,
        ghost_south,
        ghost_north,
        diagonal,
        mask_flat,
    )


def operate_flat(field_in, coeffs, side_cells):
    face_west, face_east, face_south, face_north, face_below, face_above = coeffs[:6]
    diagonal = coeffs[10]
    beside = (
        face_west * jnp.roll(field_in, 1, axis=2)
        + face_east * jnp.roll(field_in, -1, axis=2)
        + face_south * jnp.roll(field_in, 1, axis=3)
        + face_north * jnp.roll(field_in, -1, axis=3)
        + face_below * jnp.roll(field_in, side_cells, axis=3)
        + face_above * jnp.roll(field_in, -side_cells, axis=3)
    )
    return diagonal * field_in - beside


def solve_cells(source, knockdown, orient, active, ghosts):
    case_count, sub_count, side_x, flat_width = source.shape
    ply_count = orient.shape[1]
    side_cells = flat_width // ply_count
    coeffs = flat_coeffs(knockdown.astype(jnp.float32), orient, active, side_cells)
    ghost_west, ghost_east, ghost_south, ghost_north, diagonal, mask_flat = coeffs[6:]
    value_west = ghosts[:, :, :, 0:side_cells].reshape(case_count, sub_count, 1, flat_width)
    value_east = ghosts[:, :, :, side_cells : 2 * side_cells].reshape(
        case_count, sub_count, 1, flat_width
    )
    value_south = jnp.repeat(
        jnp.swapaxes(ghosts[:, :, :, 2 * side_cells : 3 * side_cells], 2, 3), side_cells, axis=3
    )
    value_north = jnp.repeat(
        jnp.swapaxes(ghosts[:, :, :, 3 * side_cells :], 2, 3), side_cells, axis=3
    )
    field_cells = source.astype(jnp.float32)
    residual = (
        mask_flat * field_cells
        + ghost_west * value_west
        + ghost_east * value_east
        + ghost_south * value_south
        + ghost_north * value_north
    )
    adjoint = jnp.zeros_like(residual)
    sigma_ratio = CHEB_CENTER / CHEB_HALF
    for sweep_index in range(SWEEPS):
        rho_now = 1.0 / sigma_ratio
        direction = residual / (CHEB_CENTER * diagonal)
        for step_index in range(STEPS):
            adjoint = adjoint + direction
            if not (sweep_index + 1 == SWEEPS and step_index + 1 == STEPS):
                residual = residual - operate_flat(direction, coeffs, side_cells)
            if step_index + 1 < STEPS:
                rho_next = 1.0 / (2.0 * sigma_ratio - rho_now)
                direction = rho_next * rho_now * direction + 2.0 * rho_next / CHEB_HALF * (
                    residual / diagonal
                )
                rho_now = rho_next
    force_west = jnp.sum(ghost_west * (value_west - adjoint), axis=2).reshape(
        case_count, sub_count, ply_count, side_cells
    )
    force_east = jnp.sum(ghost_east * (value_east - adjoint), axis=2).reshape(
        case_count, sub_count, ply_count, side_cells
    )
    south_term = (ghost_south * (value_south - adjoint)).reshape(
        case_count, sub_count, side_x, ply_count, side_cells
    )
    north_term = (ghost_north * (value_north - adjoint)).reshape(
        case_count, sub_count, side_x, ply_count, side_cells
    )
    force_south = jnp.swapaxes(jnp.sum(south_term, axis=4), 2, 3)
    force_north = jnp.swapaxes(jnp.sum(north_term, axis=4), 2, 3)
    forces = jnp.concatenate([force_west, force_east, force_south, force_north], axis=3)
    return (adjoint, forces)


def per_device(shell_state, source, knockdown, orient, active, point_owner, owner_nodes):
    case_count, sub_local, side_x, flat_width = source.shape
    ply_count = orient.shape[1]
    node_local = shell_state.shape[2]
    groups = lax.axis_size("grp")
    tile_count = lax.axis_size("sub")
    devices = groups * tile_count
    slot_depth = owner_nodes.shape[2]
    slot_total = devices * slot_depth
    boundary_width = point_owner.shape[1]
    row_count = sub_local * boundary_width
    node_table = owner_nodes[0]
    live_slot = node_table >= 0
    picked = jnp.where(
        live_slot[None, None], shell_state[:, :, jnp.where(live_slot, node_table, 0)], 0.0
    )
    owners = point_owner.reshape(row_count)
    owner_hit = (owners[:, None] == jnp.arange(devices, dtype=jnp.int32)[None, :]).astype(jnp.int32)
    slot_rank = jnp.sum((jnp.cumsum(owner_hit, axis=0) - owner_hit) * owner_hit, axis=1)
    slot_index = owners * slot_depth + slot_rank
    slot_source = (
        jnp.full((slot_total,), row_count, jnp.int32)
        .at[slot_index]
        .set(jnp.arange(row_count, dtype=jnp.int32))
    )
    arrived = lax.all_to_all(
        picked.reshape(case_count, ply_count, slot_total),
        ("grp", "sub"),
        split_axis=2,
        concat_axis=2,
        tiled=True,
    )
    values = arrived[:, :, slot_index]
    ghosts = jnp.transpose(
        values.reshape(case_count, ply_count, sub_local, boundary_width), (0, 2, 1, 3)
    )

    def solve_one(sub_index):
        sub_source = lax.dynamic_slice_in_dim(source, sub_index, 1, 1)
        sub_knock = lax.dynamic_slice_in_dim(knockdown, sub_index, 1, 0)
        sub_orient = lax.dynamic_slice_in_dim(orient, sub_index, 1, 0)
        sub_active = lax.dynamic_slice_in_dim(active, sub_index, 1, 0)
        sub_ghosts = lax.dynamic_slice_in_dim(ghosts, sub_index, 1, 1)
        return solve_cells(sub_source, sub_knock, sub_orient, sub_active, sub_ghosts)

    adjoint, forces = lax.map(solve_one, jnp.arange(sub_local))
    adjoint = jnp.moveaxis(adjoint[:, :, 0], 0, 1)
    force_rows = jnp.transpose(forces[:, :, 0], (0, 2, 3, 1)).reshape(
        sub_local * boundary_width, case_count * ply_count
    )
    force_rows = jnp.transpose(forces[:, :, 0], (0, 3, 1, 2)).reshape(
        row_count, case_count * ply_count
    )
    padded_rows = jnp.concatenate(
        [force_rows, jnp.zeros((1, case_count * ply_count), jnp.float32)], axis=0
    )
    outbound = padded_rows[slot_source].T.reshape(case_count, ply_count, slot_total)
    returned = lax.all_to_all(outbound, ("grp", "sub"), split_axis=2, concat_axis=2, tiled=True)
    returned_rows = returned.reshape(case_count * ply_count, slot_total).T
    target = jnp.where(live_slot, node_table, node_local).reshape(slot_total)
    node_rows = (
        jnp.zeros((node_local, case_count * ply_count), jnp.float32)
        .at[target]
        .add(returned_rows, mode="drop")
    )
    shell_force = node_rows.T.reshape(case_count, ply_count, node_local)
    return (adjoint, shell_force)


def solution(mesh):
    in_specs = (
        P(None, None, ("grp", "sub")),
        P(None, ("grp", "sub"), None, None),
        P(("grp", "sub"), None, None),
        P(("grp", "sub"), None),
        P(("grp", "sub")),
        P(("grp", "sub"), None),
        P(("grp", "sub"), None, None),
    )
    out_specs = (P(None, ("grp", "sub"), None, None), P(None, None, ("grp", "sub")))
    return jax.shard_map(
        per_device, mesh=mesh, in_specs=in_specs, out_specs=out_specs, check_vma=False
    )
```

profile of v0, /device:TPU:0, one launch (start us, length us, event | category | flops | bytes accessed | tf_op | source)
XLA Modules:
  0.0 206.3 jit_solution(701925207366598028)
XLA Ops:
  0.6 0.7 compare_select_fusion.2
  1.4 0.7 broadcast_compare_fusion
  2.1 10.7 %copy.32 = f32[2,48,8192]{1,0,2:T(2,128)} copy(f32[2,48,8192]{2,1,0:T(8,128)} %param.9) | data formatting | bytes 6291456 | tf_op args[0]
  12.9 6.9 %gather_fusion = f32[1024,2,48]{2,1,0:T(2,128)S(1)} fusion(f32[2,48,8192]{1,0,2:T(2,128)} %copy.32, s32[1024]{0:T(1024)S(1)} %broadcast_clamp_fusion), kind=kCustom, calls=%fused_computation | custom fusion | bytes 790528 | tf_op jit(solution)/shard_map/gather | solution.py:177
  19.8 1.0 copy.47
  20.8 0.9 copy.48
  21.8 3.7 %bitcast_select_fusion = f32[2,48,1024]{1,0,2:T(2,128)S(1)} fusion(f32[2,48,32,32]{1,0,3,2:T(2,128)S(1)} %copy.48, pred[1024]{0:T(1024)(128)(4,1)S(1)} %ge.30), kind=kLoop, calls=%fused_computation.174 | loop fusion | flops 98304 | bytes 787456 | tf_op jit(solution)/shard_map/jit(_where)/select_n | solution.py:176
  25.5 2.6 %reshape.1631 = f32[32,1,3072]{2,1,0:T(1,128)} reshape(f32[1024,2,48]{2,1,0:T(2,128)S(1)} %bitcast.161) | data formatting | bytes 786432
  28.1 7.3 %all-to-all-start = ((f32[32,1,3072]{2,1,0:T(1,128)}), f32[32,1,3072]{2,1,0:T(1,128)S(1)}, u32[]{:S(2)}, u32[]{:S(2)}) async-start(f32[32,1,3072]{2,1,0:T(1,128)} %reshape.1631), calls=%async_computation | async-start | bytes 786432 | tf_op jit(solution)/shard_map/all_to_all | solution.py:188
  35.6 1.2 reduce-window.6
  37.2 2.6 %scatter_custom_fusion = s32[1024]{0:T(1024)S(1)} fusion(s32[512]{0:T(512)S(1)} %bitcast.171, s32[512]{0:T(512)S(1)} %iota.82, s32[]{:T(128)} %constant.156.clone.1), kind=kCustom, calls=%fused_computation.194 | custom fusion | bytes 4100 | tf_op jit(solution)/shard_map/scatter | solution.py:186
  39.9 9.1 %all-to-all-done = f32[32,1,3072]{2,1,0:T(1,128)S(1)} async-done(((f32[32,1,3072]{2,1,0:T(1,128)}), f32[32,1,3072]{2,1,0:T(1,128)S(1)}, u32[]{:S(2)}, u32[]{:S(2)}) %all-to-all-start) | async-done | bytes 393248 | tf_op jit(solution)/shard_map/all_to_all | solution.py:188
  49.5 1.5 reduce.18
  51.0 1.6 reshape.1632
  52.6 2.1 %gather_fusion.1 = f32[512,2,48]{2,1,0:T(2,128)S(1)} fusion(f32[2,48,1024]{1,0,2:T(2,128)S(1)} %bitcast.168, s32[1024]{0:T(1024)S(1)} %pad_clamp_fusion), kind=kCustom, calls=%fused_computation.1 | custom fusion | bytes 395264 | tf_op jit(solution)/shard_map/gather | solution.py:195
  55.0 111.0 %while.14 = (s32[]{:T(128)}, f32[8,2,1,16,768]{4,3,0,1,2:T(8,128)}, f32[8,2,1,48,64]{3,4,1,2,0:T(8,128)S(1)}, s32[8]{0:T(128)S(1)}, s32[8]{0:T(128)S(1)}, /*inde...) while((s32[]{:T(128)}, f32[8,2,1,16,768]{4,3,0,1,2:T(8,128)}, ...), condition=%wide.region_8.9_spmd, body=%wide.region_3.8_spmd.sunk | while | flops 5484184 | bytes 18067664 | solution.py:208
  58.1 1.4 fusion.186
  63.0 0.9 broadcast_divide_fusion.6
  68.2 0.7 bitcast_dynamic-update-slice_fusion.2
  72.0 1.4 fusion.186
  76.9 0.9 broadcast_divide_fusion.6
  82.1 0.7 bitcast_dynamic-update-slice_fusion.2
  85.8 1.4 fusion.186
  90.8 0.9 broadcast_divide_fusion.6
  95.9 0.7 bitcast_dynamic-update-slice_fusion.2
  99.7 1.4 fusion.186
  104.6 0.9 broadcast_divide_fusion.6
  109.8 0.7 bitcast_dynamic-update-slice_fusion.2
  113.6 1.4 fusion.186
  118.5 0.9 broadcast_divide_fusion.6
  123.7 0.7 bitcast_dynamic-update-slice_fusion.2
  127.4 1.4 fusion.186
  132.4 0.9 broadcast_divide_fusion.6
  137.5 0.7 bitcast_dynamic-update-slice_fusion.2
  141.3 1.4 fusion.186
  146.2 0.9 broadcast_divide_fusion.6
  151.4 0.7 bitcast_dynamic-update-slice_fusion.2
  155.2 1.4 fusion.186
  160.1 0.9 broadcast_divide_fusion.6
  165.3 0.7 bitcast_dynamic-update-slice_fusion.2
  166.7 2.8 %gather_fusion.2 = f32[1024,96]{1,0:T(8,128)S(1)} fusion(f32[513,96]{1,0:T(8,128)S(1)} %concatenate.543, s32[1024]{0:T(1024)S(1)} %fusion.100), kind=kCustom, calls=%fused_computation.2 | custom fusion | bytes 790528 | tf_op jit(solution)/shard_map/gather | solution.py:219
  170.2 2.6 %reshape.1633 = f32[32,1,3072]{2,1,0:T(1,128)} reshape(f32[1024,2,48]{2,1,0:T(2,128)S(1)} %bitcast.159) | data formatting | bytes 786432
  172.8 2.8 %all-to-all-start.1 = ((f32[32,1,3072]{2,1,0:T(1,128)}), f32[32,1,3072]{2,1,0:T(1,128)S(1)}, u32[]{:S(2)}, u32[]{:S(2)}) async-start(f32[32,1,3072]{2,1,0:T(1,128)} %reshape.1633), calls=%async_computation.1 | async-start | bytes 786432 | tf_op jit(solution)/shard_map/all_to_all | solution.py:220
  175.7 13.2 %all-to-all-done.1 = f32[32,1,3072]{2,1,0:T(1,128)S(1)} async-done(((f32[32,1,3072]{2,1,0:T(1,128)}), f32[32,1,3072]{2,1,0:T(1,128)S(1)}, u32[]{:S(2)}, u32[]{:S(2)}) %all-to-all-start.1) | async-done | bytes 393248 | tf_op jit(solution)/shard_map/all_to_all | solution.py:220
  189.0 1.5 reduce.19
  190.5 1.7 reshape.1634
  192.8 8.2 %scatter_custom_fusion.1 = f32[8192,96]{1,0:T(8,128)} fusion(s32[1024]{0:T(1024)S(1)} %bitcast.174, f32[1024,96]{1,0:T(8,128)S(1)} %copy.45, f32[]{:T(128)} %constant.152.clone.1), kind=kCustom, calls=%fused_computation.172 | custom fusion | flops 98304 | bytes 3145732 | tf_op jit(solution)/shard_map/scatter-add | solution.py:226
  201.0 5.3 %copy.46 = f32[96,8192]{1,0:T(8,128)} copy(f32[96,8192]{0,1:T(8,128)} %bitcast.155) | data formatting | bytes 6291456 | tf_op jit(solution)/shard_map/transpose | solution.py:228
  (654 shorter events, 73.5 us)
Async XLA Ops:
  19.8 15.6 %copy-start.2 = (s32[8,64]{1,0:T(8,128)S(1)}, s32[8,64]{1,0:T(8,128)}, u32[]{:S(2)}) copy-start(s32[8,64]{1,0:T(8,128)} %param.14) | copy-start | bytes 6148
  21.7 33.3 %copy-start = (bf16[8,16,768]{2,1,0:T(8,128)(2,1)S(1)}, bf16[8,16,768]{2,1,0:T(8,128)(2,1)}, u32[]{:S(2)}) copy-start(bf16[8,16,768]{2,1,0:T(8,128)(2,1)} %param.11) | copy-start | bytes 589828
  21.7 33.3 %copy-start.3 = (s32[8]{0:T(128)S(1)}, s32[8]{0:T(128)}, u32[]{:S(2)}) copy-start(s32[8]{0:T(128)} %param.13) | copy-start | bytes 100
  28.1 20.9 %all-to-all-start = ((f32[32,1,3072]{2,1,0:T(1,128)}), f32[32,1,3072]{2,1,0:T(1,128)S(1)}, u32[]{:S(2)}, u32[]{:S(2)}) async-start(f32[32,1,3072]{2,1,0:T(1,128)} %reshape.1631), calls=%async_computation | async-start | bytes 786432 | tf_op jit(solution)/shard_map/all_to_all | solution.py:188
  166.7 9.0 %copy-start.1 = (s32[1,32,32]{2,1,0:T(8,128)S(1)}, s32[1,32,32]{2,1,0:T(8,128)}, u32[]{:S(2)}) copy-start(s32[1,32,32]{2,1,0:T(8,128)} %param.15) | copy-start | bytes 12292
  172.8 16.1 %all-to-all-start.1 = ((f32[32,1,3072]{2,1,0:T(1,128)}), f32[32,1,3072]{2,1,0:T(1,128)S(1)}, u32[]{:S(2)}, u32[]{:S(2)}) async-start(f32[32,1,3072]{2,1,0:T(1,128)} %reshape.1633), calls=%async_computation.1 | async-start | bytes 786432 | tf_op jit(solution)/shard_map/all_to_all | solution.py:220
where the time goes:
time: 208 us; the launch traced here: 206 us
  local copies, waits for them, and re-layouts  98.7 us (47%)
  other arithmetic  56.3 us (27%)
  waiting for transfers between devices  22.3 us (11%)
  loops' own time  18 us (9%)
  starting transfers between devices  10.1 us (5%)
    unnamed x13, local copies, waits for them, and re-layouts  19.2 us
    another operation x1, loops' own time, per_device(): adjoint, forces = lax.map(solve_one, jnp.arange(sub_local))  18 us
    all_to_all x1, waiting for transfers between devices, per_device(): lax.all_to_all(outbound, ('grp', 'sub'), split_axis=2, concat_axis=2, til...  13.2 us
    mul x8, other arithmetic, flat_coeffs(): (FIBER_COND * (1.0 - cos_square) + TRANSVERSE * cos_square) * active_mask  11.1 us
    div x32, other arithmetic, solve_cells(): direction = residual / (CHEB_CENTER * diagonal)  10.9 us
    all_to_all x1, waiting for transfers between devices, per_device(): lax.all_to_all(picked.reshape(case_count, ply_count, slot_total), ('grp',...  9.06 us
    gather x3, local copies, waits for them, and re-layouts, per_device(): shell_state[:, :, jnp.where(live_slot, node_table, 0)]  8.76 us
    scatter-add x1, other arithmetic, per_device(): node_rows = jnp.zeros((node_local, case_count * ply_count), jnp.float32)....  8.18 us
  transfers between devices with their start and end apart: 2, of which 2 were waited for; matrix products, arithmetic and copies ran while one was open for 2% of the time, Pallas kernels for 0%

commit v1 on v0

v1 whole, which is shorter than its diff:
```python
import functools
import math

import jax
import jax.numpy as jnp
from jax import lax
from jax.experimental import pallas as pl
from jax.experimental.pallas import tpu as pltpu
from jax.sharding import PartitionSpec as P

SWEEPS = 3
STEPS = 2

FIBER_COND = 1.0
TRANSVERSE = 0.25
THROUGH = 0.15
MASS_SHARE = 0.05
CHEB_CENTER = 1.02
CHEB_HALF = 0.98

LANES = 128
F32 = jnp.float32
BF16 = jnp.bfloat16


def packed_rows(slot_depth):
    return slot_depth * 3 // 4 if slot_depth % 32 == 0 else slot_depth


def pack_slots(rows_ref, out_ref, peers, slot_depth):
    if slot_depth % 32:
        out_ref[...] = rows_ref[...]
        return
    lane = lax.broadcasted_iota(jnp.int32, (8, LANES), 1)
    low = lane < 96
    for g in range(peers * slot_depth // 32):
        extra = rows_ref[g * 32 + 24 : g * 32 + 32, :]
        for k in range(3):
            shift = (96 - 32 * k) % LANES
            moved = pltpu.roll(extra, shift, 1)
            own = rows_ref[g * 32 + 8 * k : g * 32 + 8 * k + 8, :]
            out_ref[g * 24 + 8 * k : g * 24 + 8 * k + 8, :] = jnp.where(low, own, moved)


def unpack_slots(packed_ref, rows_ref, peers, slot_depth):
    if slot_depth % 32:
        rows_ref[...] = packed_ref[...]
        return
    lane = lax.broadcasted_iota(jnp.int32, (8, LANES), 1)
    for g in range(peers * slot_depth // 32):
        parts = []
        for k in range(3):
            own = packed_ref[g * 24 + 8 * k : g * 24 + 8 * k + 8, :]
            rows_ref[g * 32 + 8 * k : g * 32 + 8 * k + 8, :] = own
            parts.append(pltpu.roll(own, 32 + 32 * k, 1))
        extra = jnp.where(lane < 32, parts[0], jnp.where(lane < 64, parts[1], parts[2]))
        rows_ref[g * 32 + 24 : g * 32 + 32, :] = extra


def gather_kernel(node_ref, shell_ref, out_ref, turned, rows, *, peers, slot_depth):
    step = pl.program_id(0)
    chunk = shell_ref.shape[1]
    width = shell_ref.shape[0]
    for t in range(chunk // LANES):
        start = pl.multiple_of(step * chunk + t * LANES, LANES)
        turned[pl.ds(start, LANES), 0:width] = shell_ref[:, t * LANES : (t + 1) * LANES].T

    @pl.when(step == pl.num_programs(0) - 1)
    def _():
        def pick(group, carry):
            for u in range(16):
                slot = group * 16 + u
                node = jnp.maximum(node_ref[slot], 0)
                rows[pl.ds(slot, 1), :] = turned[pl.ds(node, 1), :]
            return carry

        lax.fori_loop(0, peers * slot_depth // 16, pick, 0)
        pack_slots(rows, out_ref, peers, slot_depth)


def gather_shell(shell_flat, nodes, peers, slot_depth):
    width, node_local = shell_flat.shape
    chunks = 8
    out_rows = peers * packed_rows(slot_depth)
    return pl.pallas_call(
        functools.partial(gather_kernel, peers=peers, slot_depth=slot_depth),
        out_shape=jax.ShapeDtypeStruct((out_rows, LANES), F32),
        grid_spec=pltpu.PrefetchScalarGridSpec(
            num_scalar_prefetch=1,
            grid=(chunks,),
            in_specs=[pl.BlockSpec((width, node_local // chunks), lambda i, n: (0, i))],
            out_specs=pl.BlockSpec((out_rows, LANES), lambda i, n: (0, 0)),
            scratch_shapes=[
                pltpu.VMEM((node_local, LANES), F32),
                pltpu.VMEM((peers * slot_depth, LANES), F32),
            ],
        ),
        compiler_params=pltpu.CompilerParams(vmem_limit_bytes=24 << 20),
        name="gather_shell",
    )(nodes, shell_flat)


def scatter_kernel(node_ref, packed_ref, out_ref, total, rows, *, peers, slot_depth):
    step = pl.program_id(0)
    chunk = out_ref.shape[1]
    width = out_ref.shape[0]
    node_local = total.shape[0] - 8

    @pl.when(step == 0)
    def _():
        unpack_slots(packed_ref, rows, peers, slot_depth)
        zero = jnp.zeros((64, LANES), F32)

        def clear(i, carry):
            total[pl.ds(pl.multiple_of(i * 64, 64), 64), :] = zero
            return carry

        lax.fori_loop(0, node_local // 64, clear, 0)
        total[node_local : node_local + 8, :] = jnp.zeros((8, LANES), F32)

        def put(group, carry):
            for u in range(8):
                slot = group * 8 + u
                node = node_ref[slot]
                node = jnp.where(node < 0, node_local, node)
                total[pl.ds(node, 1), :] += rows[pl.ds(slot, 1), :]
            return carry

        lax.fori_loop(0, peers * slot_depth // 8, put, 0)

    for t in range(chunk // LANES):
        start = pl.multiple_of(step * chunk + t * LANES, LANES)
        out_ref[:, t * LANES : (t + 1) * LANES] = total[pl.ds(start, LANES), 0:width].T


def scatter_forces(packed, nodes, peers, slot_depth, width, node_local):
    chunks = 8
    return pl.pallas_call(
        functools.partial(scatter_kernel, peers=peers, slot_depth=slot_depth),
        out_shape=jax.ShapeDtypeStruct((width, node_local), F32),
        grid_spec=pltpu.PrefetchScalarGridSpec(
            num_scalar_prefetch=1,
            grid=(chunks,),
            in_specs=[pl.BlockSpec(packed.shape, lambda i, n: (0, 0))],
            out_specs=pl.BlockSpec((width, node_local // chunks), lambda i, n: (0, i)),
            scratch_shapes=[
                pltpu.VMEM((node_local + 8, LANES), F32),
                pltpu.VMEM((peers * slot_depth, LANES), F32),
            ],
        ),
        compiler_params=pltpu.CompilerParams(vmem_limit_bytes=24 << 20),
        name="scatter_forces",
    )(nodes, packed)


def split_two(value):
    high = value.astype(BF16)
    return high, (value - high.astype(F32)).astype(BF16)


def solve_kernel(
    slot_ref, packed_ref, source_ref, knock_ref, ply_ref, spread_ref, spread_y_ref,
    fold_ref, fold_y_ref, adjoint_ref, out_ref,
    slots, bound, src, knock, face_x, face_y, face_p, diag, inverse, along_y, edge_x,
    work, resid, total, side_y, side_x, *, peers, slot_depth, plies, side,
):
    subs = 8
    cases = source_ref.shape[0]
    side_x_cells = source_ref.shape[2]
    width = source_ref.shape[3]
    tiles = width // LANES
    lane = lax.broadcasted_iota(jnp.int32, (subs, LANES), 1)
    y_place = lane % side
    first_y = y_place == 0
    last_y = y_place == side - 1
    low_ply = lane < side
    high_ply = lane >= LANES - side
    cut = [slice(t * LANES, (t + 1) * LANES) for t in range(tiles)]

    for s in range(subs):
        for t in range(tiles):
            knock[t, s * side_x_cells : (s + 1) * side_x_cells, :] = knock_ref[s, :, cut[t]].astype(F32)
            for c in range(cases):
                at = (c * subs + s) * side_x_cells
                src[t, at : at + side_x_cells, :] = source_ref[c, s, :, cut[t]].astype(F32)

    def plane(ref, x, base=0):
        return [ref[t, pl.ds(base + x, subs, stride=side_x_cells), :] for t in range(tiles)]

    def from_lower_ply(values):
        turned = [pltpu.roll(v, side, 1) for v in values]
        return [jnp.where(low_ply, turned[t - 1], turned[t]) for t in range(tiles)]

    def from_upper_ply(values):
        turned = [pltpu.roll(v, LANES - side, 1) for v in values]
        return [
            jnp.where(high_ply, turned[t + 1], turned[t]) for t in range(tiles - 1)
        ] + [turned[-1]]

    zero = jnp.zeros((subs, width), F32)
    face_x[0] = zero
    face_x[side_x_cells] = zero
    for k in range(2):
        for c in range(cases):
            work[k, c, 0] = zero
            work[k, c, side_x_cells + 1] = zero

    def faces_x(x, carry):
        here = plane(knock, x)
        there = plane(knock, x + 1)
        for t in range(tiles):
            fiber = ply_ref[0, :, cut[t]]
            face_x[x + 1, :, cut[t]] = 0.5 * (here[t] * fiber + there[t] * fiber)
        return carry

    lax.fori_loop(0, side_x_cells - 1, faces_x, 0)

    def coefficients(x, carry):
        k = plane(knock, x)
        ax = [k[t] * ply_ref[0, :, cut[t]] for t in range(tiles)]
        ay = [k[t] * ply_ref[1, :, cut[t]] for t in range(tiles)]
        ac = [k[t] * ply_ref[2, :, cut[t]] for t in range(tiles)]
        up = from_upper_ply(ac)
        fp = [ply_ref[4, :, cut[t]] * (ac[t] + up[t]) for t in range(tiles)]
        below = from_lower_ply(fp)
        at_edge = jnp.where((x == 0) | (x == side_x_cells - 1), 1.0, 0.0)
        for t in range(tiles):
            north = 0.5 * (ay[t] + pltpu.roll(ay[t], LANES - 1, 1))
            fy = jnp.where(last_y, 0.0, north)
            whole = (
                face_x[x, :, cut[t]]
                + face_x[x + 1, :, cut[t]]
                + pltpu.roll(fy, 1, 1)
                + fy
                + below[t]
                + fp[t]
                + at_edge * ax[t]
                + jnp.where(first_y | last_y, ay[t], 0.0)
                + MASS_SHARE * (ax[t] + ay[t] + ac[t])
                + (1.0 - ply_ref[3, :, cut[t]])
            )
            face_y[x, :, cut[t]] = fy
            face_p[x, :, cut[t]] = fp[t]
            diag[x, :, cut[t]] = whole
            inverse[x, :, cut[t]] = 1.0 / whole
            along_y[x, :, cut[t]] = ay[t]
        return carry

    lax.fori_loop(0, side_x_cells, coefficients, 0)
    for e, x in enumerate((0, side_x_cells - 1)):
        k = plane(knock, x)
        for t in range(tiles):
            edge_x[e, :, cut[t]] = k[t] * ply_ref[0, :, cut[t]]

    unpack_slots(packed_ref, slots, peers, slot_depth)
    points = 4 * side

    def fetch(q, carry):
        for s in range(subs):
            at = slot_ref[s * points + q]
            bound[pl.ds(q * subs + s, 1), :] = slots[pl.ds(at, 1), :]
        return carry

    lax.fori_loop(0, points, fetch, 0, unroll=4)

    rows = side * subs
    for c in range(cases):
        for e in range(2):
            high, low = split_two(bound[e * rows : (e + 1) * rows, :])
            spread = jnp.dot(
                jnp.concatenate([high, low], axis=1), spread_ref[c], preferred_element_type=F32
            )
            for t in range(tiles):
                gathered = jnp.zeros((subs, LANES), F32)
                for q in range(side):
                    part = spread[q * subs : (q + 1) * subs, cut[t]]
                    gathered = jnp.where(y_place == q, part, gathered)
                side_x[c, e, :, cut[t]] = gathered
        pieces = []
        for e in range(2, 4):
            pieces += split_two(bound[e * rows : (e + 1) * rows, :])
        side_y[c] = jnp.dot(
            jnp.concatenate(pieces, axis=1), spread_y_ref[c], preferred_element_type=F32
        )

    def residual(x, carry):
        at_first = jnp.where(x == 0, 1.0, 0.0)
        at_final = jnp.where(x == side_x_cells - 1, 1.0, 0.0)
        row = pl.multiple_of(x * subs, subs)
        for c in range(cases):
            field = plane(src, x, c * subs * side_x_cells)
            for t in range(tiles):
                value = (
                    ply_ref[3, :, cut[t]] * field[t]
                    + along_y[x, :, cut[t]] * side_y[c, pl.ds(row, subs), cut[t]]
                    + at_first * (edge_x[0, :, cut[t]] * side_x[c, 0, :, cut[t]])
                    + at_final * (edge_x[1, :, cut[t]] * side_x[c, 1, :, cut[t]])
                )
                resid[c, x, :, cut[t]] = value
                work[0, c, x + 1, :, cut[t]] = (value * inverse[x, :, cut[t]]) * (1.0 / CHEB_CENTER)
        return carry

    lax.fori_loop(0, side_x_cells, residual, 0)

    def operate(x, c, old):
        w = [work[old, c, x + 1, :, cut[t]] for t in range(tiles)]
        fp = [face_p[x, :, cut[t]] for t in range(tiles)]
        below = from_lower_ply([fp[t] * w[t] for t in range(tiles)])
        above = from_upper_ply(w)
        out = []
        for t in range(tiles):
            fy = face_y[x, :, cut[t]]
            beside = (
                face_x[x, :, cut[t]] * work[old, c, x, :, cut[t]]
                + face_x[x + 1, :, cut[t]] * work[old, c, x + 2, :, cut[t]]
                + pltpu.roll(fy * w[t], 1, 1)
                + fy * pltpu.roll(w[t], LANES - 1, 1)
                + (below[t] + fp[t] * above[t])
            )
            out.append(diag[x, :, cut[t]] * w[t] - beside)
        return w, out

    sigma = CHEB_CENTER / CHEB_HALF
    rho_first = 1.0 / sigma
    rho_next = 1.0 / (2.0 * sigma - rho_first)
    keep = rho_next * rho_first
    gain = 2.0 * rho_next / CHEB_HALF

    for sweep in range(SWEEPS):
        final = sweep == SWEEPS - 1

        def second(x, carry, sweep=sweep, final=final):
            for c in range(cases):
                w, moved = operate(x, c, 0)
                for t in range(tiles):
                    r = resid[c, x, :, cut[t]] - moved[t]
                    later = keep * w[t] + gain * (r * inverse[x, :, cut[t]])
                    sums = w[t] + later
                    if sweep:
                        sums = total[c, x, :, cut[t]] + sums
                    total[c, x, :, cut[t]] = sums
                    if not final:
                        resid[c, x, :, cut[t]] = r
                        work[1, c, x + 1, :, cut[t]] = later
            return carry

        lax.fori_loop(0, side_x_cells, second, 0)
        if final:
            break

        def first(x, carry):
            for c in range(cases):
                _, moved = operate(x, c, 1)
                for t in range(tiles):
                    r = resid[c, x, :, cut[t]] - moved[t]
                    resid[c, x, :, cut[t]] = r
                    work[0, c, x + 1, :, cut[t]] = (r * inverse[x, :, cut[t]]) * (1.0 / CHEB_CENTER)
            return carry

        lax.fori_loop(0, side_x_cells, first, 0)

    def force_y(x, carry):
        row = pl.multiple_of(x * subs, subs)
        for c in range(cases):
            for t in range(tiles):
                value = total[c, x, :, cut[t]]
                src[t, pl.ds(c * subs * side_x_cells + x, subs, stride=side_x_cells), :] = value
                side_y[c, pl.ds(row, subs), cut[t]] = along_y[x, :, cut[t]] * (
                    side_y[c, pl.ds(row, subs), cut[t]] - value
                )
        return carry

    lax.fori_loop(0, side_x_cells, force_y, 0)
    for t in range(tiles):
        adjoint_ref[:, cut[t]] = src[t]

    sums_x = [jnp.zeros((rows, LANES), F32) for _ in range(2)]
    sums_y = jnp.zeros((rows, 2 * LANES), F32)
    for c in range(cases):
        for piece in split_two(side_y[c]):
            sums_y = sums_y + jnp.dot(piece, fold_y_ref[c], preferred_element_type=F32)
        for e, x in enumerate((0, side_x_cells - 1)):
            at_ply = edge_x[e] * (side_x[c, e] - total[c, x])
            y_wide = lax.broadcasted_iota(jnp.int32, (subs, width), 1) % side
            for piece in split_two(at_ply):
                wide = piece.astype(F32)
                tall = jnp.concatenate(
                    [jnp.where(y_wide == q, wide, 0.0) for q in range(side)], axis=0
                ).astype(BF16)
                sums_x[e] = sums_x[e] + jnp.dot(tall, fold_ref[c], preferred_element_type=F32)
    bound[0:rows, :] = sums_x[0]
    bound[rows : 2 * rows, :] = sums_x[1]
    bound[2 * rows : 3 * rows, :] = sums_y[:, :LANES]
    bound[3 * rows : 4 * rows, :] = sums_y[:, LANES:]

    def post(q, carry):
        for s in range(subs):
            at = slot_ref[s * points + q]
            slots[pl.ds(at, 1), :] = bound[pl.ds(q * subs + s, 1), :]
        return carry

    lax.fori_loop(0, points, post, 0, unroll=4)
    pack_slots(slots, out_ref, peers, slot_depth)


def solve_block(packed, slot_index, source, knockdown, ply_terms, tables, peers, slot_depth):
    cases, subs, side_x, width = source.shape
    plies = width // side_x
    side = width // plies
    vm = pl.BlockSpec(memory_space=pltpu.VMEM)
    out_rows = peers * packed_rows(slot_depth)
    planes = (side_x, subs, width)
    scratch = [
        pltpu.VMEM((peers * slot_depth, LANES), F32),
        pltpu.VMEM((4 * side * subs, LANES), F32),
        pltpu.VMEM((width // LANES, cases * subs * side_x, LANES), F32),
        pltpu.VMEM((width // LANES, subs * side_x, LANES), F32),
        pltpu.VMEM((side_x + 1, subs, width), F32),
        pltpu.VMEM(planes, F32),
        pltpu.VMEM(planes, F32),
        pltpu.VMEM(planes, F32),
        pltpu.VMEM(planes, F32),
        pltpu.VMEM(planes, F32),
        pltpu.VMEM((2, subs, width), F32),
        pltpu.VMEM((2, cases, side_x + 2, subs, width), F32),
        pltpu.VMEM((cases,) + planes, F32),
        pltpu.VMEM((cases,) + planes, F32),
        pltpu.VMEM((cases, side_x * subs, width), F32),
        pltpu.VMEM((cases, 2, subs, width), F32),
    ]
    adjoint, outbound = pl.pallas_call(
        functools.partial(
            solve_kernel, peers=peers, slot_depth=slot_depth, plies=plies, side=side
        ),
        out_shape=(
            jax.ShapeDtypeStruct((cases * subs * side_x, width), F32),
            jax.ShapeDtypeStruct((out_rows, LANES), F32),
        ),
        in_specs=[pl.BlockSpec(memory_space=pltpu.SMEM)] + [vm] * 8,
        out_specs=(vm, vm),
        scratch_shapes=scratch,
        compiler_params=pltpu.CompilerParams(vmem_limit_bytes=32 << 20),
        name="solve_block",
    )(slot_index, packed, source, knockdown, ply_terms, *tables)
    return adjoint.reshape(source.shape), outbound


def ply_table(orient, active, side):
    plies = orient.shape[1]
    index = jnp.arange(plies)[None, :]
    mask = (index < active[:, None]).astype(F32)
    upper = ((index + 1 < active[:, None]) & (index + 1 < plies)).astype(F32)
    cos_square = jnp.cos(orient.astype(F32) * (math.pi / 6.0)) ** 2
    fiber = (FIBER_COND * cos_square + TRANSVERSE * (1.0 - cos_square)) * mask
    cross = (FIBER_COND * (1.0 - cos_square) + TRANSVERSE * cos_square) * mask
    terms = jnp.stack([fiber, cross, THROUGH * mask, mask, 0.5 * upper])
    return jnp.repeat(terms, side, axis=2)


def spread_tables(cases, plies, side):
    width = plies * side
    lane = jnp.arange(LANES)[:, None]
    cell = jnp.arange(width)[None, :]
    spread, spread_y, fold, fold_y = [], [], [], []
    for c in range(cases):
        hit = lane == c * plies + cell // side
        at_south = hit & (cell % side == 0)
        at_north = hit & (cell % side == side - 1)
        spread.append(jnp.concatenate([hit, hit], axis=0))
        spread_y.append(jnp.concatenate([at_south, at_south, at_north, at_north], axis=0))
        fold.append(hit.T)
        fold_y.append(jnp.concatenate([at_south.T, at_north.T], axis=1))
    return [jnp.stack(m).astype(BF16) for m in (spread, spread_y, fold, fold_y)]


def per_device(shell_state, source, knockdown, orient, active, point_owner, owner_nodes):
    cases, subs, side_x, width = source.shape
    plies = orient.shape[1]
    side = width // plies
    node_local = shell_state.shape[2]
    peers = owner_nodes.shape[1]
    slot_depth = owner_nodes.shape[2]
    axes = ("grp", "sub")
    per_peer = packed_rows(slot_depth)

    nodes = owner_nodes.reshape(peers * slot_depth)
    picked = gather_shell(
        shell_state.reshape(cases * plies, node_local), nodes, peers, slot_depth
    )
    arrived = lax.all_to_all(
        picked.reshape(peers, per_peer, LANES), axes, split_axis=0, concat_axis=0, tiled=True
    )

    owners = point_owner.reshape(-1)
    place = jnp.arange(owners.shape[0])
    earlier = (owners[:, None] == owners[None, :]) & (place[None, :] < place[:, None])
    slot_index = owners * slot_depth + jnp.sum(earlier.astype(jnp.int32), axis=1)

    adjoint, outbound = solve_block(
        arrived.reshape(peers * per_peer, LANES), slot_index, source, knockdown,
        ply_table(orient, active, side), spread_tables(cases, plies, side), peers, slot_depth,
    )
    returned = lax.all_to_all(
        outbound.reshape(peers, per_peer, LANES), axes, split_axis=0, concat_axis=0, tiled=True
    )
    force = scatter_forces(
        returned.reshape(peers * per_peer, LANES), nodes, peers, slot_depth,
        cases * plies, node_local,
    )
    return adjoint, force.reshape(cases, plies, node_local)


def solution(mesh):
    in_specs = (
        P(None, None, ("grp", "sub")),
        P(None, ("grp", "sub"), None, None),
        P(("grp", "sub"), None, None),
        P(("grp", "sub"), None),
        P(("grp", "sub")),
        P(("grp", "sub"), None),
        P(("grp", "sub"), None, None),
    )
    out_specs = (P(None, ("grp", "sub"), None, None), P(None, None, ("grp", "sub")))
    return jax.shard_map(
        per_device, mesh=mesh, in_specs=in_specs, out_specs=out_specs, check_vma=False
    )
```

time: 208 us -> 78.7 us (0.38)
  local copies, waits for them, and re-layouts: 98.7 us -> 8.65 us
  other arithmetic: 56.3 us -> 6.72 us
  Pallas kernels: 0 us -> 34.5 us
  loops' own time: 18 us -> 0 us
  waiting for transfers between devices: 22.3 us -> 4.55 us
  blocking collectives: 0 us -> 15.6 us
  starting transfers between devices: 10.1 us -> 7.3 us
    pallas_call x0 -> x3, Pallas kernels: none -> 34.5 us  [the longest x1 19.1 us: solve_block(): pl.pallas_call(functools.partial(solve_kernel, peers=peers, slot_depth=sl...]
    another operation x1 -> x0, loops' own time: 18 us -> none  [per_device(): adjoint, forces = lax.map(solve_one, jnp.arange(sub_local))]
    all_to_all x2 -> x1, waiting for transfers between devices: 22.3 us -> 4.55 us  [per_device(): lax.all_to_all(picked.reshape(peers, per_peer, LANES), axes, split_axis=0...]
    slice x288 -> x0, local copies, waits for them, and re-layouts: 16.2 us -> none  [the longest x80 6.38 us: operate_flat(): jnp.roll(field_in, 1, axis=3)]
    all_to_all x0 -> x1, blocking collectives: none -> 15.6 us  [per_device(): lax.all_to_all(outbound.reshape(peers, per_peer, LANES), axes, split_axis...]
    gather x5 -> x0, local copies, waits for them, and re-layouts: 13.7 us -> none  [the longest x3 8.76 us: per_device(): shell_state[:, :, jnp.where(live_slot, node_table, 0)]]
    unnamed x13 -> x16, local copies, waits for them, and re-layouts: 19.2 us -> 5.72 us
    mul x49 -> x0, other arithmetic: 13.1 us -> none  [the longest x8 11.1 us: flat_coeffs(): (FIBER_COND * (1.0 - cos_square) + TRANSVERSE * cos_square) * active_mask]
  transfers between devices with their start and end apart: 2 -> 1, of which waited for: 2 -> 1; matrix products, arithmetic and copies ran while one was open for 2% -> 11% of each run, Pallas kernels for 0% -> 0%
where the time goes in v1:
time: 78.7 us; the launch traced here: 78.1 us
  Pallas kernels  34.5 us (44%)
  blocking collectives  15.6 us (20%)
  local copies, waits for them, and re-layouts  8.65 us (11%)
  starting transfers between devices  7.3 us (9%)
  other arithmetic  6.72 us (9%)
  waiting for transfers between devices  4.55 us (6%)
  between operations  0.8 us (1%)
    pallas_call x1, Pallas kernels, solve_block(): pl.pallas_call(functools.partial(solve_kernel, peers=peers, slot_depth=sl...  19.1 us
    all_to_all x1, blocking collectives, per_device(): lax.all_to_all(outbound.reshape(peers, per_peer, LANES), axes, split_axis...  15.6 us
    pallas_call x1, Pallas kernels, scatter_forces(): pl.pallas_call(functools.partial(scatter_kernel, peers=peers, slot_depth=...  10.3 us
    all_to_all x1, starting transfers between devices, per_device(): lax.all_to_all(picked.reshape(peers, per_peer, LANES), axes, split_axis=0...  7.3 us
    unnamed x16, local copies, waits for them, and re-layouts  5.72 us
    pallas_call x1, Pallas kernels, gather_shell(): pl.pallas_call(functools.partial(gather_kernel, peers=peers, slot_depth=s...  5.1 us
    all_to_all x1, waiting for transfers between devices, per_device(): lax.all_to_all(picked.reshape(peers, per_peer, LANES), axes, split_axis=0...  4.55 us
    unnamed x4, other arithmetic  2.63 us
  transfers between devices with their start and end apart: 1, of which 1 were waited for; matrix products, arithmetic and copies ran while one was open for 11% of the time, Pallas kernels for 0%

profile of v1, /device:TPU:0, one launch (start us, length us, event | category | flops | bytes accessed | tf_op | source)
XLA Modules:
  0.0 78.1 jit_solution(5496211433403183633)
XLA Ops:
  0.6 0.0 copy-start.6
  0.6 0.0 copy-start.5
  0.7 0.8 %reshape.281.node_ref = s32[1024]{0:T(1024)S(1)} reshape(s32[1,32,32]{2,1,0:T(8,128)} %param.13) | data formatting | bytes 8192 | tf_op jit(solution)/shard_map/reshape | solution.py:486
  1.4 0.0 copy-start
  1.5 1.9 %copy-done = f32[2,48,8192]{2,1,0:T(8,128)S(1)} copy-done((f32[2,48,8192]{2,1,0:T(8,128)S(1)}, f32[2,48,8192]{2,1,0:T(8,128)}, u32[]{:S(2)}) %copy-start) | copy-done | bytes 3145752
  3.3 5.1 %gather_shell.1 = f32[768,128]{1,0:T(8,128)} custom-call(s32[1024]{0:T(1024)S(1)} %reshape.281.node_ref, f32[96,8192]{1,0:T(8,128)S(1)} %bitcast.25), custom_call_target="tpu_custom_call" | custom-call | tf_op jit(solution)/shard_map/gather_shell/pallas_call | solution.py:85
  8.4 0.0 copy-start.7
  8.4 7.3 %all-to-all-start = ((f32[32,24,128]{2,1,0:T(8,128)}), f32[32,24,128]{2,1,0:T(8,128)S(1)}, u32[]{:S(2)}, u32[]{:S(2)}) async-start(f32[32,24,128]{2,1,0:T(8,128)} %bitcast.1), calls=%async_computation | async-start | bytes 786432 | tf_op jit(solution)/shard_map/all_to_all | solution.py:490
  15.8 0.3 iota_compare_fusion.3
  16.1 0.8 fusion.2
  16.9 0.3 fusion.8
  17.2 0.0 copy-done.6
  17.2 0.0 copy-done.5
  17.2 0.7 constant_dynamic-update-slice_fusion.4
  17.9 0.6 constant_dynamic-update-slice_fusion.3
  18.5 0.7 constant_dynamic-update-slice_fusion.2
  19.2 0.7 constant_dynamic-update-slice_fusion.1
  19.8 0.1 add_bitcast_fusion.4
  20.0 0.2 add_convert_fusion.2.fold_y_ref
  20.1 0.1 add_bitcast_fusion.2
  20.2 0.1 add_convert_fusion.1.spread_ref
  20.3 0.7 constant_dynamic-update-slice_fusion
  21.0 0.8 %add_convert_fusion.3.fold_ref = bf16[2,768,128]{2,1,0:T(8,128)(2,1)} fusion(pred[1,768,128]{2,1,0:T(8,128)(4,1)S(1)} %get-tuple-element.25, pred[1,768,128]{2,1,0:T(8,128)(4,1)S(1)} %get-tuple-element.26), kind=kLoop, calls=%fused_computation.10 | loop fusion | flops 393216 | bytes 589824 | tf_op jit(solution)/shard_map/convert_element_type | solution.py:473
  21.8 0.0 copy-done.7
  21.8 0.1 reshape.280
  21.9 1.0 %broadcast_in_dim.2 = f32[5,8,48,16]{3,2,1,0:T(8,128)S(1)} broadcast(f32[5,8,48]{2,1,0:T(8,128)} %constant_dynamic-update-slice_fusion), dimensions={0,1,2} | broadcast | bytes 130560 | tf_op jit(solution)/shard_map/broadcast_in_dim | solution.py:457
  22.9 1.0 %reshape.285.ply_ref = f32[5,8,768]{2,1,0:T(8,128)} reshape(f32[5,8,48,16]{3,2,1,0:T(8,128)S(1)} %broadcast_in_dim.2) | data formatting | bytes 245760 | tf_op jit(solution)/shard_map/reshape | solution.py:457
  23.9 0.2 convert_reduce_fusion
  24.2 0.2 add_bitcast_fusion
  24.4 0.3 add_convert_fusion.spread_y_ref
  24.7 4.5 %all-to-all-done = f32[32,24,128]{2,1,0:T(8,128)S(1)} async-done(((f32[32,24,128]{2,1,0:T(8,128)}), f32[32,24,128]{2,1,0:T(8,128)S(1)}, u32[]{:S(2)}, u32[]{:S(2)}) %all-to-all-start) | async-done | bytes 393248 | tf_op jit(solution)/shard_map/all_to_all | solution.py:490
  29.3 0.0 copy-start.1
  29.3 1.0 %copy-done.1 = bf16[2,768,128]{2,1,0:T(8,128)(2,1)S(1)} copy-done((bf16[2,768,128]{2,1,0:T(8,128)(2,1)S(1)}, bf16[2,768,128]{2,1,0:T(8,128)(2,1)}, u32[]{:S(2)}) %copy-start.1) | copy-done | bytes 393240
  30.3 0.0 copy-start.2
  30.3 0.9 %copy-done.2 = f32[5,8,768]{2,1,0:T(8,128)S(1)} copy-done((f32[5,8,768]{2,1,0:T(8,128)S(1)}, f32[5,8,768]{2,1,0:T(8,128)}, u32[]{:S(2)}) %copy-start.2) | copy-done | bytes 122904
  31.2 0.0 copy-start.3
  31.2 1.0 %copy-done.3 = bf16[2,8,16,768]{3,2,1,0:T(8,128)(2,1)S(1)} copy-done((bf16[2,8,16,768]{3,2,1,0:T(8,128)(2,1)S(1)}, bf16[2,8,16,768]{3,2,1,0:T(8,128)(2,1)}, u32[]{:S(2)}) %copy-start.3) | copy-done | bytes 393240
  32.2 0.0 copy-start.4
  32.2 0.9 %copy-done.4 = bf16[8,16,768]{2,1,0:T(8,128)(2,1)S(1)} copy-done((bf16[8,16,768]{2,1,0:T(8,128)(2,1)S(1)}, bf16[8,16,768]{2,1,0:T(8,128)(2,1)}, u32[]{:S(2)}) %copy-start.4) | copy-done | bytes 196632
  33.1 19.1 %solve_block.1 = (f32[256,768]{1,0:T(8,128)}, f32[768,128]{1,0:T(8,128)S(1)}) custom-call(s32[512]{0:T(512)S(1)} %multiply_add_fusion.slot_ref, f32[768,128]{1,0:T(8,128)S(1)} %bitcast.26, bf16[2,8,16,768]{3,2,1,0:T(8,128)(2,1)S(1)} %copy-done.3, bf16[8,16,768]{2,1,0:T(8,128)(2,1)S(1)} %copy-done.4, f32[5,8,768]{2,1,0:T(8,128)S(1)} %copy-done.2, ...), custom_call_target="tpu_custom_call" | custom-call | tf_op jit(solution)/shard_map/solve_block/pallas_call | solution.py:431
  52.2 15.6 %all_to_all.10 = f32[32,24,128]{2,1,0:T(8,128)S(1)} all-to-all(f32[32,24,128]{2,1,0:T(8,128)S(1)} %bitcast.28), channel_id=1, replica_groups=mesh['grp'=4,'sub'=8] {'grp','sub'}, dimensions={0} | all-to-all | bytes 786432 | tf_op jit(solution)/shard_map/all_to_all | solution.py:503
  67.8 10.3 %scatter_forces.1 = f32[96,8192]{1,0:T(8,128)} custom-call(s32[1024]{0:T(1024)S(1)} %reshape.281.node_ref, f32[768,128]{1,0:T(8,128)S(1)} %bitcast.27), custom_call_target="tpu_custom_call" | custom-call | tf_op jit(solution)/shard_map/scatter_forces/pallas_call | solution.py:138
  (7 shorter events, 0.0 us)
Async XLA Ops:
  0.6 16.5 %copy-start.6 = (s32[8]{0:T(128)S(1)}, s32[8]{0:T(128)}, u32[]{:S(2)}) copy-start(s32[8]{0:T(128)} %param.11) | copy-start | bytes 100
  0.6 16.5 %copy-start.5 = (s32[8,48]{1,0:T(8,128)S(1)}, s32[8,48]{1,0:T(8,128)}, u32[]{:S(2)}) copy-start(s32[8,48]{1,0:T(8,128)} %param.10) | copy-start | bytes 4612
  1.4 1.9 %copy-start = (f32[2,48,8192]{2,1,0:T(8,128)S(1)}, f32[2,48,8192]{2,1,0:T(8,128)}, u32[]{:S(2)}) copy-start(f32[2,48,8192]{2,1,0:T(8,128)} %param.7) | copy-start | bytes 9437188
  8.4 13.4 %copy-start.7 = (s32[8,64]{1,0:T(8,128)S(1)}, s32[8,64]{1,0:T(8,128)}, u32[]{:S(2)}) copy-start(s32[8,64]{1,0:T(8,128)} %param.12) | copy-start | bytes 6148
  8.4 20.8 %all-to-all-start = ((f32[32,24,128]{2,1,0:T(8,128)}), f32[32,24,128]{2,1,0:T(8,128)S(1)}, u32[]{:S(2)}, u32[]{:S(2)}) async-start(f32[32,24,128]{2,1,0:T(8,128)} %bitcast.1), calls=%async_computation | async-start | bytes 786432 | tf_op jit(solution)/shard_map/all_to_all | solution.py:490
  29.3 1.0 %copy-start.1 = (bf16[2,768,128]{2,1,0:T(8,128)(2,1)S(1)}, bf16[2,768,128]{2,1,0:T(8,128)(2,1)}, u32[]{:S(2)}) copy-start(bf16[2,768,128]{2,1,0:T(8,128)(2,1)} %add_convert_fusion.3.fold_ref) | copy-start | bytes 1179652
  30.3 0.9 %copy-start.2 = (f32[5,8,768]{2,1,0:T(8,128)S(1)}, f32[5,8,768]{2,1,0:T(8,128)}, u32[]{:S(2)}) copy-start(f32[5,8,768]{2,1,0:T(8,128)} %reshape.285.ply_ref) | copy-start | bytes 368644
  31.2 1.0 %copy-start.3 = (bf16[2,8,16,768]{3,2,1,0:T(8,128)(2,1)S(1)}, bf16[2,8,16,768]{3,2,1,0:T(8,128)(2,1)}, u32[]{:S(2)}) copy-start(bf16[2,8,16,768]{3,2,1,0:T(8,128)(2,1)} %source_ref.1) | copy-start | bytes 1179652
  32.2 0.9 %copy-start.4 = (bf16[8,16,768]{2,1,0:T(8,128)(2,1)S(1)}, bf16[8,16,768]{2,1,0:T(8,128)(2,1)}, u32[]{:S(2)}) copy-start(bf16[8,16,768]{2,1,0:T(8,128)(2,1)} %knock_ref.1) | copy-start | bytes 589828

commit v2 on v1

v2 whole, which is shorter than its diff:
```python
import functools
import math

import jax
import jax.numpy as jnp
from jax import lax
from jax.experimental import pallas as pl
from jax.experimental.pallas import tpu as pltpu
from jax.sharding import PartitionSpec as P

SWEEPS = 3
STEPS = 2

FIBER_COND = 1.0
TRANSVERSE = 0.25
THROUGH = 0.15
MASS_SHARE = 0.05
CHEB_CENTER = 1.02
CHEB_HALF = 0.98

LANES = 128
HALF = 64
F32 = jnp.float32
BF16 = jnp.bfloat16


def packed_rows(slot_depth):
    return slot_depth * 3 // 4 if slot_depth % 32 == 0 else slot_depth


def pack_slots(rows_ref, out_ref, peers, slot_depth):
    used = lax.broadcasted_iota(jnp.int32, (8, LANES), 1) % HALF < 48
    if slot_depth % 32:
        for g in range(peers * slot_depth // 8):
            part = slice(g * 8, g * 8 + 8)
            out_ref[part, :] = jnp.where(used, rows_ref[part, :], 0.0)
        return
    for g in range(peers * slot_depth // 32):
        extra = rows_ref[g * 32 + 24 : g * 32 + 32, :]
        for k in range(3):
            moved = pltpu.roll(extra, 48 - 16 * k, 1)
            own = rows_ref[g * 32 + 8 * k : g * 32 + 8 * k + 8, :]
            out_ref[g * 24 + 8 * k : g * 24 + 8 * k + 8, :] = jnp.where(used, own, moved)


def unpack_slots(packed_ref, rows_ref, peers, slot_depth):
    if slot_depth % 32:
        rows_ref[...] = packed_ref[...]
        return
    third = lax.broadcasted_iota(jnp.int32, (8, LANES), 1) % HALF // 16
    for g in range(peers * slot_depth // 32):
        parts = []
        for k in range(3):
            own = packed_ref[g * 24 + 8 * k : g * 24 + 8 * k + 8, :]
            rows_ref[g * 32 + 8 * k : g * 32 + 8 * k + 8, :] = own
            parts.append(pltpu.roll(own, LANES - 48 + 16 * k, 1))
        extra = jnp.where(third == 0, parts[0], jnp.where(third == 1, parts[1], parts[2]))
        rows_ref[g * 32 + 24 : g * 32 + 32, :] = extra


def gather_kernel(node_ref, shell_hbm, out_ref, shell, turned, rows, sems, *, peers, slot_depth):
    width, node_local = shell.shape
    chunks = sems.shape[0]
    chunk = node_local // chunks
    copies = []
    for i in range(chunks):
        part = slice(i * chunk, (i + 1) * chunk)
        copies.append(pltpu.make_async_copy(shell_hbm.at[:, part], shell.at[:, part], sems.at[i]))
        copies[i].start()
    gap = jnp.zeros((HALF - width // 2, LANES), F32)
    for i in range(chunks):
        copies[i].wait()
        for t in range(i * chunk // LANES, (i + 1) * chunk // LANES):
            tile = shell[:, t * LANES : (t + 1) * LANES]
            parts = [tile[: width // 2], gap, tile[width // 2 :], gap]
            turned[8 + t * LANES : 8 + (t + 1) * LANES, :] = jnp.concatenate(parts, axis=0).T
    turned[0:8, :] = turned[8:16, :]

    def pick(peer, carry):
        for u in range(slot_depth):
            slot = peer * slot_depth + u
            rows[pl.ds(slot, 1), :] = turned[pl.ds(node_ref[peer, u] + 8, 1), :]
        return carry

    lax.fori_loop(0, peers, pick, 0)
    pack_slots(rows, out_ref, peers, slot_depth)


def gather_shell(shell_flat, nodes):
    width, node_local = shell_flat.shape
    peers, slot_depth = nodes.shape
    chunks = 8
    out_rows = peers * packed_rows(slot_depth)
    return pl.pallas_call(
        functools.partial(gather_kernel, peers=peers, slot_depth=slot_depth),
        out_shape=jax.ShapeDtypeStruct((out_rows, LANES), F32),
        in_specs=[
            pl.BlockSpec(memory_space=pltpu.SMEM),
            pl.BlockSpec(memory_space=pltpu.HBM),
        ],
        out_specs=pl.BlockSpec(memory_space=pltpu.VMEM),
        scratch_shapes=[
            pltpu.VMEM((width, node_local), F32),
            pltpu.VMEM((node_local + 8, LANES), F32),
            pltpu.VMEM((peers * slot_depth, LANES), F32),
            pltpu.SemaphoreType.DMA((chunks,)),
        ],
        name="gather_shell",
    )(nodes, shell_flat)


def scatter_kernel(node_ref, packed_ref, out_hbm, total, rows, out, sems, *, peers, slot_depth):
    width, node_local = out.shape
    unpack_slots(packed_ref, rows, peers, slot_depth)
    zero = jnp.zeros((64, LANES), F32)
    total[0:8, :] = jnp.zeros((8, LANES), F32)

    def clear(i, carry):
        total[pl.ds(pl.multiple_of(8 + i * 64, 8), 64), :] = zero
        return carry

    lax.fori_loop(0, node_local // 64, clear, 0)

    def put(peer, carry):
        for u in range(slot_depth):
            slot = peer * slot_depth + u
            total[pl.ds(node_ref[peer, u] + 8, 1), :] += rows[pl.ds(slot, 1), :]
        return carry

    lax.fori_loop(0, peers, put, 0)

    chunks = sems.shape[0]
    chunk = node_local // chunks
    copies = []
    for i in range(chunks):
        for t in range(i * chunk // LANES, (i + 1) * chunk // LANES):
            tile = total[8 + t * LANES : 8 + (t + 1) * LANES, :].T
            out[: width // 2, t * LANES : (t + 1) * LANES] = tile[: width // 2]
            out[width // 2 :, t * LANES : (t + 1) * LANES] = tile[HALF : HALF + width // 2]
        part = slice(i * chunk, (i + 1) * chunk)
        copies.append(pltpu.make_async_copy(out.at[:, part], out_hbm.at[:, part], sems.at[i]))
        copies[i].start()
    for i in range(chunks):
        copies[i].wait()


def scatter_forces(packed, nodes, width, node_local):
    peers, slot_depth = nodes.shape
    chunks = 8
    return pl.pallas_call(
        functools.partial(scatter_kernel, peers=peers, slot_depth=slot_depth),
        out_shape=jax.ShapeDtypeStruct((width, node_local), F32),
        in_specs=[
            pl.BlockSpec(memory_space=pltpu.SMEM),
            pl.BlockSpec(memory_space=pltpu.VMEM),
        ],
        out_specs=pl.BlockSpec(memory_space=pltpu.HBM),
        scratch_shapes=[
            pltpu.VMEM((node_local + 8, LANES), F32),
            pltpu.VMEM((peers * slot_depth, LANES), F32),
            pltpu.VMEM((width, node_local), F32),
            pltpu.SemaphoreType.DMA((chunks,)),
        ],
        name="scatter_forces",
    )(nodes, packed)


def split_two(value):
    high = value.astype(BF16)
    return high, (value - high.astype(F32)).astype(BF16)


def from_lower_ply(values, low_ply, side):
    turned = [pltpu.roll(v, side, 1) for v in values]
    return [jnp.where(low_ply, turned[t - 1], turned[t]) for t in range(len(values))]


def from_upper_ply(values, high_ply, side):
    turned = [pltpu.roll(v, LANES - side, 1) for v in values]
    return [
        jnp.where(high_ply, turned[t + 1], turned[t]) for t in range(len(values) - 1)
    ] + [turned[-1]]


def prepare_kernel(
    source_ref, knock_ref, cosine_ref, active_ref, slot_col_ref, slot_row_ref,
    planes_hbm, field_hbm, turned_hit_hbm, edge_x, hit_ref, spread_ref, fold_ref, fold_y_ref,
    planes, field, turned_hit_ref, src, knock, ply_ref, sems, *, plies, side,
):
    cases, subs, cells_x, width = source_ref.shape
    tiles = width // LANES
    lane = lax.broadcasted_iota(jnp.int32, (subs, LANES), 1)
    y_place = lane % side
    first_y = y_place == 0
    last_y = y_place == side - 1
    low_ply = lane < side
    high_ply = lane >= LANES - side
    cut = [slice(t * LANES, (t + 1) * LANES) for t in range(tiles)]

    def indicator(condition):
        return jnp.where(condition, 1.0, 0.0).astype(BF16)

    tall = spread_ref.shape[1]
    row = lax.broadcasted_iota(jnp.int32, (tall, width), 0) % LANES - HALF
    cell = lax.broadcasted_iota(jnp.int32, (tall, width), 1)
    own = row == cell // side
    y_cell = cell % side
    spread_ref[0] = indicator(own)
    spread_ref[1] = indicator(own & (y_cell == 0))
    spread_ref[2] = indicator(own & (y_cell == side - 1))
    cell = lax.broadcasted_iota(jnp.int32, (width, LANES), 0)
    own = lax.broadcasted_iota(jnp.int32, (width, LANES), 1) == cell // side
    y_cell = cell % side
    fold_ref[...] = indicator(own)
    fold_y_ref[:, :LANES] = indicator(own & (y_cell == 0))
    fold_y_ref[:, LANES:] = indicator(own & (y_cell == side - 1))

    rows, slots = hit_ref.shape
    hit_ref[...] = indicator(
        lax.broadcasted_iota(jnp.int32, (rows, slots), 1) == slot_col_ref[...]
    )
    turned_hit_ref[...] = indicator(
        lax.broadcasted_iota(jnp.int32, (slots, rows), 0) == slot_row_ref[...]
    )
    turned_copy = pltpu.make_async_copy(turned_hit_ref, turned_hit_hbm, sems.at[0])
    turned_copy.start()

    ply = lax.broadcasted_iota(jnp.int32, (subs, LANES), 1)
    mask = jnp.where(ply < active_ref[...], 1.0, 0.0)
    upper = jnp.where((ply + 1 < active_ref[...]) & (ply + 1 < plies), 0.5, 0.0)
    cos_square = cosine_ref[...]
    terms = jnp.concatenate(
        [
            (FIBER_COND * cos_square + TRANSVERSE * (1.0 - cos_square)) * mask,
            (FIBER_COND * (1.0 - cos_square) + TRANSVERSE * cos_square) * mask,
            mask,
            upper,
        ],
        axis=0,
    )
    high, low = split_two(terms)
    only = spread_ref[0, HALF : HALF + LANES, :]
    spread_terms = jnp.dot(high, only, preferred_element_type=F32) + jnp.dot(
        low, only, preferred_element_type=F32
    )
    for k in range(4):
        ply_ref[k] = spread_terms[k * subs : (k + 1) * subs, :]

    for s in range(subs):
        for t in range(tiles):
            knock[t, s * cells_x : (s + 1) * cells_x, :] = knock_ref[s, :, cut[t]].astype(F32)
            for c in range(cases):
                at = (c * subs + s) * cells_x
                src[t, at : at + cells_x, :] = source_ref[c, s, :, cut[t]].astype(F32)

    def plane(ref, x, base=0):
        return [ref[t, pl.ds(base + x, subs, stride=cells_x), :] for t in range(tiles)]

    face_x, face_y, face_p, diag, inverse, along_y = (planes.at[k] for k in range(6))
    face_x[0] = jnp.zeros((subs, width), F32)
    face_x[cells_x] = jnp.zeros((subs, width), F32)

    def faces_x(x, carry):
        here = plane(knock, x)
        there = plane(knock, x + 1)
        for t in range(tiles):
            fiber = ply_ref[0, :, cut[t]]
            face_x[x + 1, :, cut[t]] = 0.5 * (here[t] * fiber + there[t] * fiber)
        return carry

    lax.fori_loop(0, cells_x - 1, faces_x, 0)

    def coefficients(x, carry):
        k = plane(knock, x)
        ax = [k[t] * ply_ref[0, :, cut[t]] for t in range(tiles)]
        ay = [k[t] * ply_ref[1, :, cut[t]] for t in range(tiles)]
        ac = [k[t] * (THROUGH * ply_ref[2, :, cut[t]]) for t in range(tiles)]
        up = from_upper_ply(ac, high_ply, side)
        fp = [ply_ref[3, :, cut[t]] * (ac[t] + up[t]) for t in range(tiles)]
        below = from_lower_ply(fp, low_ply, side)
        at_edge = jnp.where((x == 0) | (x == cells_x - 1), 1.0, 0.0)
        for t in range(tiles):
            fy = jnp.where(last_y, 0.0, 0.5 * (ay[t] + pltpu.roll(ay[t], LANES - 1, 1)))
            whole = (
                face_x[x, :, cut[t]]
                + face_x[x + 1, :, cut[t]]
                + pltpu.roll(fy, 1, 1)
                + fy
                + below[t]
                + fp[t]
                + at_edge * ax[t]
                + jnp.where(first_y | last_y, ay[t], 0.0)
                + MASS_SHARE * (ax[t] + ay[t] + ac[t])
                + (1.0 - ply_ref[2, :, cut[t]])
            )
            face_y[x, :, cut[t]] = fy
            face_p[x, :, cut[t]] = fp[t]
            diag[x, :, cut[t]] = whole
            inverse[x, :, cut[t]] = 1.0 / whole
            along_y[x, :, cut[t]] = ay[t]
            for c in range(cases):
                value = src[t, pl.ds(c * subs * cells_x + x, subs, stride=cells_x), :]
                field[c, x, :, cut[t]] = ply_ref[2, :, cut[t]] * value
        return carry

    lax.fori_loop(0, cells_x, coefficients, 0)
    copies = [
        pltpu.make_async_copy(planes, planes_hbm, sems.at[1]),
        pltpu.make_async_copy(field, field_hbm, sems.at[2]),
    ]
    for copy in copies:
        copy.start()
    for e, x in enumerate((0, cells_x - 1)):
        k = plane(knock, x)
        for t in range(tiles):
            edge_x[e, :, cut[t]] = k[t] * ply_ref[0, :, cut[t]]
    for copy in [turned_copy] + copies:
        copy.wait()


def prepare(source, knockdown, orient, active, slot_index, slots):
    cases, subs, cells_x, width = source.shape
    plies = orient.shape[1]
    side = width // plies
    rows = slot_index.shape[0]
    cosine = jnp.cos(orient.astype(F32) * (math.pi / 6.0)) ** 2
    cosine = jnp.pad(cosine, ((0, 0), (0, LANES - plies)))
    slot_turned = slot_index.reshape(subs, rows // subs).T.reshape(rows)
    planes = (6, cells_x + 1, subs, width)
    field = (cases, cells_x, subs, width)
    vm = pl.BlockSpec(memory_space=pltpu.VMEM)
    hbm = pl.BlockSpec(memory_space=pltpu.HBM)
    shapes = [
        (planes, F32),
        (field, F32),
        ((slots, rows), BF16),
        ((2, subs, width), F32),
        ((rows, slots), BF16),
        ((3, 2 * LANES + HALF, width), BF16),
        ((width, LANES), BF16),
        ((width, 2 * LANES), BF16),
    ]
    return pl.pallas_call(
        functools.partial(prepare_kernel, plies=plies, side=side),
        out_shape=[jax.ShapeDtypeStruct(*shape) for shape in shapes],
        in_specs=[vm] * 6,
        out_specs=[hbm] * 3 + [vm] * 5,
        scratch_shapes=[
            pltpu.VMEM(planes, F32),
            pltpu.VMEM(field, F32),
            pltpu.VMEM((slots, rows), BF16),
            pltpu.VMEM((width // LANES, cases * subs * cells_x, LANES), F32),
            pltpu.VMEM((width // LANES, subs * cells_x, LANES), F32),
            pltpu.VMEM((4, subs, width), F32),
            pltpu.SemaphoreType.DMA((3,)),
        ],
        cost_estimate=pl.CostEstimate(
            flops=40_000_000, bytes_accessed=12_000_000, transcendentals=0
        ),
        name="prepare",
    )(source, knockdown, cosine, active[:, None], slot_turned[:, None], slot_turned[None, :])


def solve_kernel(
    packed_ref, planes_hbm, field_hbm, turned_hit_hbm, edge_x, hit_ref, spread_ref, fold_ref,
    fold_y_ref, total_hbm, out_ref,
    planes, field, turned_hit_ref, total, slots, bound, work, resid, side_y, side_x, sems,
    *, peers, slot_depth, side,
):
    copies = [
        pltpu.make_async_copy(field_hbm, field, sems.at[0]),
        pltpu.make_async_copy(planes_hbm, planes, sems.at[1]),
        pltpu.make_async_copy(turned_hit_hbm, turned_hit_ref, sems.at[2]),
    ]
    for copy in copies:
        copy.start()
    face_x, face_y, face_p, diag, inverse, along_y = (planes.at[k] for k in range(6))
    cases, cells_x, subs, width = field.shape
    tiles = width // LANES
    lane = lax.broadcasted_iota(jnp.int32, (subs, LANES), 1)
    y_place = lane % side
    low_ply = lane < side
    high_ply = lane >= LANES - side
    cut = [slice(t * LANES, (t + 1) * LANES) for t in range(tiles)]

    zero = jnp.zeros((subs, width), F32)
    for k in range(2):
        for c in range(cases):
            work[k, c, 0] = zero
            work[k, c, cells_x + 1] = zero

    unpack_slots(packed_ref, slots, peers, slot_depth)
    pieces = jnp.concatenate(split_two(slots[...]), axis=1)
    bound[...] = jnp.dot(hit_ref[...], pieces, preferred_element_type=F32).astype(BF16)

    rows = side * subs
    for c in range(cases):
        own = slice((1 - c) * HALF, (1 - c) * HALF + 2 * LANES)
        for e in range(2):
            spread = jnp.dot(
                bound[e * rows : (e + 1) * rows, :],
                spread_ref[0, own, :],
                preferred_element_type=F32,
            )
            for t in range(tiles):
                gathered = spread[0:subs, cut[t]]
                for q in range(1, side):
                    part = spread[q * subs : (q + 1) * subs, cut[t]]
                    gathered = jnp.where(y_place == q, part, gathered)
                side_x[c, e, :, cut[t]] = gathered
        side_y[c] = jnp.dot(
            bound[2 * rows : 3 * rows, :], spread_ref[1, own, :], preferred_element_type=F32
        ) + jnp.dot(
            bound[3 * rows : 4 * rows, :], spread_ref[2, own, :], preferred_element_type=F32
        )
    for copy in copies[:2]:
        copy.wait()

    def residual(x, carry):
        at_first = jnp.where(x == 0, 1.0, 0.0)
        at_final = jnp.where(x == cells_x - 1, 1.0, 0.0)
        row = pl.multiple_of(x * subs, subs)
        for c in range(cases):
            for t in range(tiles):
                value = (
                    field[c, x, :, cut[t]]
                    + along_y[x, :, cut[t]] * side_y[c, pl.ds(row, subs), cut[t]]
                    + at_first * (edge_x[0, :, cut[t]] * side_x[c, 0, :, cut[t]])
                    + at_final * (edge_x[1, :, cut[t]] * side_x[c, 1, :, cut[t]])
                )
                resid[c, x, :, cut[t]] = value
                work[0, c, x + 1, :, cut[t]] = (value * inverse[x, :, cut[t]]) * (1.0 / CHEB_CENTER)
        return carry

    lax.fori_loop(0, cells_x, residual, 0, unroll=4)

    def operate(x, c, old):
        w = [work[old, c, x + 1, :, cut[t]] for t in range(tiles)]
        fp = [face_p[x, :, cut[t]] for t in range(tiles)]
        below = from_lower_ply([fp[t] * w[t] for t in range(tiles)], low_ply, side)
        above = from_upper_ply(w, high_ply, side)
        out = []
        for t in range(tiles):
            fy = face_y[x, :, cut[t]]
            beside = (
                face_x[x, :, cut[t]] * work[old, c, x, :, cut[t]]
                + face_x[x + 1, :, cut[t]] * work[old, c, x + 2, :, cut[t]]
                + pltpu.roll(fy * w[t], 1, 1)
                + fy * pltpu.roll(w[t], LANES - 1, 1)
                + (below[t] + fp[t] * above[t])
            )
            out.append(diag[x, :, cut[t]] * w[t] - beside)
        return w, out

    sigma = CHEB_CENTER / CHEB_HALF
    rho_first = 1.0 / sigma
    rho_next = 1.0 / (2.0 * sigma - rho_first)
    keep = rho_next * rho_first
    gain = 2.0 * rho_next / CHEB_HALF

    for sweep in range(SWEEPS):
        final = sweep == SWEEPS - 1

        def second(x, carry, sweep=sweep, final=final):
            for c in range(cases):
                w, moved = operate(x, c, 0)
                for t in range(tiles):
                    r = resid[c, x, :, cut[t]] - moved[t]
                    later = keep * w[t] + gain * (r * inverse[x, :, cut[t]])
                    sums = w[t] + later
                    if sweep:
                        sums = total[c, x, :, cut[t]] + sums
                    total[c, x, :, cut[t]] = sums
                    if not final:
                        resid[c, x, :, cut[t]] = r
                        work[1, c, x + 1, :, cut[t]] = later
                    else:
                        row = pl.multiple_of(x * subs, subs)
                        side_y[c, pl.ds(row, subs), cut[t]] = along_y[x, :, cut[t]] * (
                            side_y[c, pl.ds(row, subs), cut[t]] - sums
                        )
            return carry

        lax.fori_loop(0, cells_x, second, 0, unroll=True)
        if final:
            break

        def first(x, carry):
            for c in range(cases):
                _, moved = operate(x, c, 1)
                for t in range(tiles):
                    r = resid[c, x, :, cut[t]] - moved[t]
                    resid[c, x, :, cut[t]] = r
                    work[0, c, x + 1, :, cut[t]] = (r * inverse[x, :, cut[t]]) * (1.0 / CHEB_CENTER)
            return carry

        lax.fori_loop(0, cells_x, first, 0, unroll=True)

    total_copy = pltpu.make_async_copy(total, total_hbm, sems.at[3])
    total_copy.start()

    y_wide = lax.broadcasted_iota(jnp.int32, (subs, width), 1) % side
    lower = lax.broadcasted_iota(jnp.int32, (rows, LANES), 1) < HALF
    sums = []
    for c in range(cases):
        sums_y = jnp.zeros((rows, 2 * LANES), F32)
        for piece in split_two(side_y[c]):
            sums_y = sums_y + jnp.dot(piece, fold_y_ref[...], preferred_element_type=F32)
        sums_x = []
        for e, x in enumerate((0, cells_x - 1)):
            at_ply = edge_x[e] * (side_x[c, e] - total[c, x])
            folded = jnp.zeros((rows, LANES), F32)
            for piece in split_two(at_ply):
                wide = piece.astype(F32)
                tall = jnp.concatenate(
                    [jnp.where(y_wide == q, wide, 0.0) for q in range(side)], axis=0
                ).astype(BF16)
                folded = folded + jnp.dot(tall, fold_ref[...], preferred_element_type=F32)
            sums_x.append(folded)
        sums.append(sums_x + [sums_y[:, :LANES], sums_y[:, LANES:]])
    for e in range(4):
        both = jnp.where(lower, sums[0][e], pltpu.roll(sums[1][e], HALF, 1))
        bound[e * rows : (e + 1) * rows, :] = jnp.concatenate(split_two(both), axis=1)
    copies[2].wait()
    posted = jnp.dot(turned_hit_ref[...], bound[...], preferred_element_type=F32)
    slots[...] = posted[:, :LANES] + posted[:, LANES:]
    pack_slots(slots, out_ref, peers, slot_depth)
    total_copy.wait()


def solve_block(packed, ready, peers, slot_depth, side):
    cases, cells_x, subs, width = ready[1].shape
    vm = pl.BlockSpec(memory_space=pltpu.VMEM)
    hbm = pl.BlockSpec(memory_space=pltpu.HBM)
    out_rows = peers * packed_rows(slot_depth)
    planes = (cells_x, subs, width)
    return pl.pallas_call(
        functools.partial(solve_kernel, peers=peers, slot_depth=slot_depth, side=side),
        out_shape=(
            jax.ShapeDtypeStruct((cases,) + planes, F32),
            jax.ShapeDtypeStruct((out_rows, LANES), F32),
        ),
        in_specs=[vm] + [hbm] * 3 + [vm] * 5,
        out_specs=(hbm, vm),
        scratch_shapes=[
            pltpu.VMEM(ready[0].shape, F32),
            pltpu.VMEM(ready[1].shape, F32),
            pltpu.VMEM(ready[2].shape, BF16),
            pltpu.VMEM((cases,) + planes, F32),
            pltpu.VMEM((peers * slot_depth, LANES), F32),
            pltpu.VMEM((4 * side * subs, 2 * LANES), BF16),
            pltpu.VMEM((2, cases, cells_x + 2, subs, width), F32),
            pltpu.VMEM((cases,) + planes, F32),
            pltpu.VMEM((cases, cells_x * subs, width), F32),
            pltpu.VMEM((cases, 2, subs, width), F32),
            pltpu.SemaphoreType.DMA((4,)),
        ],
        name="solve_block",
    )(packed, *ready)


def per_device(shell_state, source, knockdown, orient, active, point_owner, owner_nodes):
    cases, subs, side_x, width = source.shape
    plies = orient.shape[1]
    side = width // plies
    node_local = shell_state.shape[2]
    _, peers, slot_depth = owner_nodes.shape
    axes = ("grp", "sub")
    per_peer = packed_rows(slot_depth)

    nodes = owner_nodes.reshape(peers, slot_depth)
    picked = gather_shell(shell_state.reshape(cases * plies, node_local), nodes)
    arrived = lax.all_to_all(
        picked.reshape(peers, per_peer, LANES), axes, split_axis=0, concat_axis=0, tiled=True
    )

    owners = point_owner.reshape(-1)
    place = jnp.arange(owners.shape[0])
    earlier = (owners[:, None] == owners[None, :]) & (place[None, :] < place[:, None])
    slot_index = owners * slot_depth + jnp.sum(earlier.astype(jnp.int32), axis=1)
    ready = prepare(source, knockdown, orient, active, slot_index, peers * slot_depth)

    planes, outbound = solve_block(
        arrived.reshape(peers * per_peer, LANES), ready, peers, slot_depth, side
    )
    returned = lax.all_to_all(
        outbound.reshape(peers, per_peer, LANES), axes, split_axis=0, concat_axis=0, tiled=True
    )
    adjoint = jnp.transpose(planes, (0, 2, 1, 3))
    force = scatter_forces(
        returned.reshape(peers * per_peer, LANES), nodes, cases * plies, node_local
    )
    return adjoint, force.reshape(cases, plies, node_local)


def solution(mesh):
    in_specs = (
        P(None, None, ("grp", "sub")),
        P(None, ("grp", "sub"), None, None),
        P(("grp", "sub"), None, None),
        P(("grp", "sub"), None),
        P(("grp", "sub")),
        P(("grp", "sub"), None),
        P(("grp", "sub"), None, None),
    )
    out_specs = (P(None, ("grp", "sub"), None, None), P(None, None, ("grp", "sub")))
    return jax.shard_map(
        per_device, mesh=mesh, in_specs=in_specs, out_specs=out_specs, check_vma=False
    )
```

time: 78.7 us -> 66.4 us (0.84)
  blocking collectives: 15.6 us -> 0 us
  waiting for transfers between devices: 4.55 us -> 12.3 us
  other arithmetic: 6.72 us -> 0.3 us
  starting transfers between devices: 7.3 us -> 12.2 us
  local copies, waits for them, and re-layouts: 8.65 us -> 6.8 us
  Pallas kernels: 34.5 us -> 33.6 us
    all_to_all x1 -> x0, blocking collectives: 15.6 us -> none  [per_device(): lax.all_to_all(outbound.reshape(peers, per_peer, LANES), axes, split_axis...]
    all_to_all x0 -> x1, waiting for transfers between devices: none -> 11.3 us  [per_device(): lax.all_to_all(outbound.reshape(peers, per_peer, LANES), axes, split_axis...]
    pallas_call x0 -> x1, Pallas kernels: none -> 9.21 us  [prepare(): pl.pallas_call(functools.partial(prepare_kernel, plies=plies, side=side),...]
    pallas_call x1, Pallas kernels: 19.1 us -> 10.2 us  [solve_block(): pl.pallas_call(functools.partial(solve_kernel, peers=peers, slot_depth=sl...]
    all_to_all x0 -> x1, starting transfers between devices: none -> 4.88 us  [per_device(): lax.all_to_all(outbound.reshape(peers, per_peer, LANES), axes, split_axis...]
    all_to_all x1, waiting for transfers between devices: 4.55 us -> 0.98 us  [per_device(): lax.all_to_all(picked.reshape(peers, per_peer, LANES), axes, split_axis=0...]
    unnamed x4 -> x0, other arithmetic: 2.63 us -> none
    unnamed x16 -> x11, local copies, waits for them, and re-layouts: 5.72 us -> 3.78 us
  transfers between devices with their start and end apart: 1 -> 2, of which waited for: 1 -> 2; matrix products, arithmetic and copies ran while one was open for 11% -> 8% of each run, Pallas kernels for 0% -> 14%
where the time goes in v2:
time: 66.4 us; the launch traced here: 65.8 us
  Pallas kernels  33.6 us (51%)
  waiting for transfers between devices  12.3 us (19%)
  starting transfers between devices  12.2 us (18%)
  local copies, waits for them, and re-layouts  6.8 us (10%)
  between operations  0.71 us (1%)
    all_to_all x1, waiting for transfers between devices, per_device(): lax.all_to_all(outbound.reshape(peers, per_peer, LANES), axes, split_axis...  11.3 us
    pallas_call x1, Pallas kernels, solve_block(): pl.pallas_call(functools.partial(solve_kernel, peers=peers, slot_depth=sl...  10.2 us
    pallas_call x1, Pallas kernels, prepare(): pl.pallas_call(functools.partial(prepare_kernel, plies=plies, side=side),...  9.21 us
    pallas_call x1, Pallas kernels, scatter_forces(): pl.pallas_call(functools.partial(scatter_kernel, peers=peers, slot_depth=...  8.45 us
    all_to_all x1, starting transfers between devices, per_device(): lax.all_to_all(picked.reshape(peers, per_peer, LANES), axes, split_axis=0...  7.3 us
    pallas_call x1, Pallas kernels, gather_shell(): pl.pallas_call(functools.partial(gather_kernel, peers=peers, slot_depth=s...  5.68 us
    all_to_all x1, starting transfers between devices, per_device(): lax.all_to_all(outbound.reshape(peers, per_peer, LANES), axes, split_axis...  4.88 us
    unnamed x11, local copies, waits for them, and re-layouts  3.78 us
  transfers between devices with their start and end apart: 2, of which 2 were waited for; matrix products, arithmetic and copies ran while one was open for 8% of the time, Pallas kernels for 14%

profile of v2, /device:TPU:0, one launch (start us, length us, event | category | flops | bytes accessed | tf_op | source)
XLA Modules:
  0.0 65.8 jit_solution(3289580962038730953)
XLA Ops:
  0.6 0.0 copy-start.2
  0.6 0.0 copy-start.4
  0.7 0.0 copy-start.3
  0.7 5.7 %gather_shell.1 = f32[768,128]{1,0:T(8,128)} custom-call(s32[32,32]{1,0:T(8,128)} %bitcast.18, f32[96,8192]{1,0:T(8,128)} %bitcast.11), custom_call_target="tpu_custom_call" | custom-call | tf_op jit(solution)/shard_map/gather_shell/pallas_call | solution.py:94
  6.3 7.3 %all-to-all-start = ((f32[32,24,128]{2,1,0:T(8,128)}), f32[32,24,128]{2,1,0:T(8,128)S(1)}, u32[]{:S(2)}, u32[]{:S(2)}) async-start(f32[32,24,128]{2,1,0:T(8,128)} %bitcast.13), calls=%async_computation | async-start | bytes 786432 | tf_op jit(solution)/shard_map/all_to_all | solution.py:573
  13.7 0.0 copy-done.2
  13.7 0.1 eq.15
  13.7 0.3 convert_reduce_fusion
  14.0 0.1 reduce_sum.12
  14.1 0.1 copy.18
  14.2 0.7 %broadcast_in_dim_reshape.9.slot_row_ref = s32[1,512]{1,0:T(1,128)} reshape(s32[64,8]{1,0:T(8,128)S(1)} %copy.18) | data formatting | bytes 4096 | tf_op jit(solution)/shard_map/broadcast_in_dim;reshape | solution.py:361
  14.9 0.8 %broadcast_in_dim_reshape.10.slot_col_ref = s32[512,1]{1,0:T(8,128)} reshape(s32[64,8]{1,0:T(8,128)S(1)} %copy.18) | data formatting | bytes 4096 | tf_op jit(solution)/shard_map/broadcast_in_dim;reshape | solution.py:361
  15.7 0.0 copy-done.4
  15.7 0.7 %copy.20.active_ref = s32[8,1]{1,0:T(8,128)} copy(s32[8,1]{0,1:T(1,128)S(1)} %bitcast.20) | data formatting | bytes 64 | tf_op jit(solution)/shard_map/broadcast_in_dim | solution.py:361
  16.4 0.0 copy-done.3
  16.4 0.6 pad.4.cosine_ref
  17.0 9.2 %prepare.1 = (f32[6,17,8,768]{3,2,1,0:T(8,128)}, f32[2,16,8,768]{3,2,1,0:T(8,128)}, bf16[1024,512]{1,0:T(8,128)(2,1)}, f32[2,8,768]{2,1,0:T(8,128)}, bf16[512,10...) custom-call(bf16[2,8,16,768]{3,2,1,0:T(8,128)(2,1)} %source_ref.1, ...), custom_call_target="tpu_custom_call" | custom-call | flops 40000000 | bytes 12000000 | tf_op jit(solution)/shard_map/prepare/pallas_call | solution.py:343
  26.2 1.0 %all-to-all-done = f32[32,24,128]{2,1,0:T(8,128)S(1)} async-done(((f32[32,24,128]{2,1,0:T(8,128)}), f32[32,24,128]{2,1,0:T(8,128)S(1)}, u32[]{:S(2)}, u32[]{:S(2)}) %all-to-all-start) | async-done | bytes 393248 | tf_op jit(solution)/shard_map/all_to_all | solution.py:573
  27.2 0.0 copy-start.1
  27.2 0.8 %copy-done.1 = f32[32,24,128]{2,1,0:T(8,128)} copy-done((f32[32,24,128]{2,1,0:T(8,128)}, f32[32,24,128]{2,1,0:T(8,128)S(1)}, u32[]{:S(2)}) %copy-start.1) | copy-done | bytes 393240
  28.0 10.2 %solve_block.1 = (f32[2,16,8,768]{3,2,1,0:T(8,128)}, f32[768,128]{1,0:T(8,128)}) custom-call(f32[768,128]{1,0:T(8,128)} %bitcast.15, f32[6,17,8,768]{3,2,1,0:T(8,128)} %get-tuple-element.12.planes_hbm, f32[2,16,8,768]{3,2,1,0:T(8,128)} %get-tuple-element.13.field_hbm, bf16[1024,512]{1,0:T(8,128)(2,1)} %get-tuple-element.14.turned_hit_hbm, ...), custom_call_target="tpu_custom_call" | custom-call | tf_op jit(solution)/shard_map/solve_block/pallas_call | solution.py:537
  38.2 4.9 %all-to-all-start.1 = ((f32[32,24,128]{2,1,0:T(8,128)}), f32[32,24,128]{2,1,0:T(8,128)S(1)}, u32[]{:S(2)}, u32[]{:S(2)}) async-start(f32[32,24,128]{2,1,0:T(8,128)} %bitcast.17), calls=%async_computation.1 | async-start | bytes 786432 | tf_op jit(solution)/shard_map/all_to_all | solution.py:586
  43.1 2.2 %copy.22 = f32[2,8,16,768]{3,2,1,0:T(8,128)} copy(f32[2,8,16,768]{3,1,2,0:T(8,128)} %bitcast.16) | data formatting | bytes 1572864
  45.4 11.3 %all-to-all-done.1 = f32[32,24,128]{2,1,0:T(8,128)S(1)} async-done(((f32[32,24,128]{2,1,0:T(8,128)}), f32[32,24,128]{2,1,0:T(8,128)S(1)}, u32[]{:S(2)}, u32[]{:S(2)}) %all-to-all-start.1) | async-done | bytes 393248 | tf_op jit(solution)/shard_map/all_to_all | solution.py:586
  56.6 0.0 copy-start
  56.6 0.7 %copy-done = f32[32,24,128]{2,1,0:T(8,128)} copy-done((f32[32,24,128]{2,1,0:T(8,128)}, f32[32,24,128]{2,1,0:T(8,128)S(1)}, u32[]{:S(2)}) %copy-start) | copy-done | bytes 393240
  57.4 8.5 %scatter_forces.1 = f32[96,8192]{1,0:T(8,128)} custom-call(s32[32,32]{1,0:T(8,128)} %bitcast.19, f32[768,128]{1,0:T(8,128)} %bitcast.14), custom_call_target="tpu_custom_call" | custom-call | tf_op jit(solution)/shard_map/scatter_forces/pallas_call | solution.py:150
  (2 shorter events, 0.1 us)
Async XLA Ops:
  0.6 13.0 %copy-start.2 = (s32[8,64]{1,0:T(8,128)S(1)}, s32[8,64]{1,0:T(8,128)}, u32[]{:S(2)}) copy-start(s32[8,64]{1,0:T(8,128)} %param.12) | copy-start | bytes 6148
  0.6 15.0 %copy-start.4 = (s32[8]{0:T(128)S(1)}, s32[8]{0:T(128)}, u32[]{:S(2)}) copy-start(s32[8]{0:T(128)} %param.11) | copy-start | bytes 100
  0.7 15.7 %copy-start.3 = (s32[8,48]{1,0:T(8,128)S(1)}, s32[8,48]{1,0:T(8,128)}, u32[]{:S(2)}) copy-start(s32[8,48]{1,0:T(8,128)} %param.10) | copy-start | bytes 4612
  6.3 20.9 %all-to-all-start = ((f32[32,24,128]{2,1,0:T(8,128)}), f32[32,24,128]{2,1,0:T(8,128)S(1)}, u32[]{:S(2)}, u32[]{:S(2)}) async-start(f32[32,24,128]{2,1,0:T(8,128)} %bitcast.13), calls=%async_computation | async-start | bytes 786432 | tf_op jit(solution)/shard_map/all_to_all | solution.py:573
  27.2 0.8 %copy-start.1 = (f32[32,24,128]{2,1,0:T(8,128)}, f32[32,24,128]{2,1,0:T(8,128)S(1)}, u32[]{:S(2)}) copy-start(f32[32,24,128]{2,1,0:T(8,128)S(1)} %all-to-all-done) | copy-start | bytes 1179652
  38.2 18.4 %all-to-all-start.1 = ((f32[32,24,128]{2,1,0:T(8,128)}), f32[32,24,128]{2,1,0:T(8,128)S(1)}, u32[]{:S(2)}, u32[]{:S(2)}) async-start(f32[32,24,128]{2,1,0:T(8,128)} %bitcast.17), calls=%async_computation.1 | async-start | bytes 786432 | tf_op jit(solution)/shard_map/all_to_all | solution.py:586
  56.6 0.7 %copy-start = (f32[32,24,128]{2,1,0:T(8,128)}, f32[32,24,128]{2,1,0:T(8,128)S(1)}, u32[]{:S(2)}) copy-start(f32[32,24,128]{2,1,0:T(8,128)S(1)} %all-to-all-done.1) | copy-start | bytes 1179652

commit v3 on v2

--- a/solution.py
+++ b/solution.py
@@ -109,22 +109,52 @@
     )(nodes, shell_flat)
 
 
-def scatter_kernel(node_ref, packed_ref, out_hbm, total, rows, out, sems, *, peers, slot_depth):
+def pair_kernel(node_turned_ref, node_row_ref, node_ref, same_ref, node_out_ref):
+    depth, peers = node_turned_ref.shape
+    node_out_ref[...] = node_ref[...]
+    for peer in range(peers):
+        column = node_turned_ref[:, peer : peer + 1]
+        same_ref[peer * depth : (peer + 1) * depth, :] = jnp.where(
+            column == node_row_ref[...], 1.0, 0.0
+        ).astype(BF16)
+
+
+def pair_slots(nodes):
+    peers, slot_depth = nodes.shape
+    slots = peers * slot_depth
+    vm = pl.BlockSpec(memory_space=pltpu.VMEM)
+    return pl.pallas_call(
+        pair_kernel,
+        out_shape=[
+            jax.ShapeDtypeStruct((slots, slots), BF16),
+            jax.ShapeDtypeStruct(nodes.shape, jnp.int32),
+        ],
+        in_specs=[vm] * 3,
+        out_specs=[vm] * 2,
+        compiler_params=pltpu.CompilerParams(vmem_limit_bytes=16 << 20),
+        cost_estimate=pl.CostEstimate(
+            flops=4_000_000, bytes_accessed=4_000_000, transcendentals=0
+        ),
+        name="pair_slots",
+    )(nodes.T, nodes.reshape(1, slots), nodes)
+
+
+def scatter_kernel(
+    node_ref, same_ref, packed_ref, out_hbm, total, rows, out, sems, *, peers, slot_depth
+):
     width, node_local = out.shape
     unpack_slots(packed_ref, rows, peers, slot_depth)
-    zero = jnp.zeros((64, LANES), F32)
-    total[0:8, :] = jnp.zeros((8, LANES), F32)
-
-    def clear(i, carry):
-        total[pl.ds(pl.multiple_of(8 + i * 64, 8), 64), :] = zero
-        return carry
-
-    lax.fori_loop(0, node_local // 64, clear, 0)
+    pieces = jnp.concatenate(split_two(rows[...]), axis=1)
+    zero = jnp.zeros((LANES, LANES), F32)
+    for t in range(node_local // LANES):
+        total[8 + t * LANES : 8 + (t + 1) * LANES, :] = zero
+    summed = jnp.dot(same_ref[...], pieces, preferred_element_type=F32)
+    rows[...] = summed[:, :LANES] + summed[:, LANES:]
 
     def put(peer, carry):
         for u in range(slot_depth):
             slot = peer * slot_depth + u
-            total[pl.ds(node_ref[peer, u] + 8, 1), :] += rows[pl.ds(slot, 1), :]
+            total[pl.ds(node_ref[peer, u] + 8, 1), :] = rows[pl.ds(slot, 1), :]
         return carry
 
     lax.fori_loop(0, peers, put, 0)
@@ -140,20 +170,18 @@
         part = slice(i * chunk, (i + 1) * chunk)
         copies.append(pltpu.make_async_copy(out.at[:, part], out_hbm.at[:, part], sems.at[i]))
         copies[i].start()
-    for i in range(chunks):
-        copies[i].wait()
-
-
-def scatter_forces(packed, nodes, width, node_local):
+    for copy in copies:
+        copy.wait()
+
+
+def scatter_forces(packed, same, nodes, width, node_local):
     peers, slot_depth = nodes.shape
     chunks = 8
+    vm = pl.BlockSpec(memory_space=pltpu.VMEM)
     return pl.pallas_call(
         functools.partial(scatter_kernel, peers=peers, slot_depth=slot_depth),
         out_shape=jax.ShapeDtypeStruct((width, node_local), F32),
-        in_specs=[
-            pl.BlockSpec(memory_space=pltpu.SMEM),
-            pl.BlockSpec(memory_space=pltpu.VMEM),
-        ],
+        in_specs=[pl.BlockSpec(memory_space=pltpu.SMEM), vm, vm],
         out_specs=pl.BlockSpec(memory_space=pltpu.HBM),
         scratch_shapes=[
             pltpu.VMEM((node_local + 8, LANES), F32),
@@ -161,8 +189,9 @@
             pltpu.VMEM((width, node_local), F32),
             pltpu.SemaphoreType.DMA((chunks,)),
         ],
+        compiler_params=pltpu.CompilerParams(vmem_limit_bytes=40 << 20),
         name="scatter_forces",
-    )(nodes, packed)
+    )(nodes, same, packed)
 
 
 def split_two(value):
@@ -182,10 +211,19 @@
     ] + [turned[-1]]
 
 
+def ply_spread(tall, width, side):
+    row = lax.broadcasted_iota(jnp.int32, (tall, width), 0)
+    cell = lax.broadcasted_iota(jnp.int32, (tall, width), 1)
+    return row, cell % side, row % HALF == cell // side
+
+
+def indicator(condition):
+    return jnp.where(condition, 1.0, 0.0).astype(BF16)
+
+
 def prepare_kernel(
-    source_ref, knock_ref, cosine_ref, active_ref, slot_col_ref, slot_row_ref,
-    planes_hbm, field_hbm, turned_hit_hbm, edge_x, hit_ref, spread_ref, fold_ref, fold_y_ref,
-    planes, field, turned_hit_ref, src, knock, ply_ref, sems, *, plies, side,
+    active_ref, source_ref, knock_ref, cosine_ref, planes_hbm,
+    planes, src, knock, ply_ref, sems, *, plies, side,
 ):
     cases, subs, cells_x, width = source_ref.shape
     tiles = width // LANES
@@ -197,37 +235,13 @@
     high_ply = lane >= LANES - side
     cut = [slice(t * LANES, (t + 1) * LANES) for t in range(tiles)]
 
-    def indicator(condition):
-        return jnp.where(condition, 1.0, 0.0).astype(BF16)
-
-    tall = spread_ref.shape[1]
-    row = lax.broadcasted_iota(jnp.int32, (tall, width), 0) % LANES - HALF
-    cell = lax.broadcasted_iota(jnp.int32, (tall, width), 1)
-    own = row == cell // side
-    y_cell = cell % side
-    spread_ref[0] = indicator(own)
-    spread_ref[1] = indicator(own & (y_cell == 0))
-    spread_ref[2] = indicator(own & (y_cell == side - 1))
-    cell = lax.broadcasted_iota(jnp.int32, (width, LANES), 0)
-    own = lax.broadcasted_iota(jnp.int32, (width, LANES), 1) == cell // side
-    y_cell = cell % side
-    fold_ref[...] = indicator(own)
-    fold_y_ref[:, :LANES] = indicator(own & (y_cell == 0))
-    fold_y_ref[:, LANES:] = indicator(own & (y_cell == side - 1))
-
-    rows, slots = hit_ref.shape
-    hit_ref[...] = indicator(
-        lax.broadcasted_iota(jnp.int32, (rows, slots), 1) == slot_col_ref[...]
-    )
-    turned_hit_ref[...] = indicator(
-        lax.broadcasted_iota(jnp.int32, (slots, rows), 0) == slot_row_ref[...]
-    )
-    turned_copy = pltpu.make_async_copy(turned_hit_ref, turned_hit_hbm, sems.at[0])
-    turned_copy.start()
-
-    ply = lax.broadcasted_iota(jnp.int32, (subs, LANES), 1)
-    mask = jnp.where(ply < active_ref[...], 1.0, 0.0)
-    upper = jnp.where((ply + 1 < active_ref[...]) & (ply + 1 < plies), 0.5, 0.0)
+    ply = lax.broadcasted_iota(jnp.int32, (subs, plies), 1)
+    sub = lax.broadcasted_iota(jnp.int32, (subs, plies), 0)
+    present = jnp.zeros((subs, plies), jnp.int32)
+    for s in range(subs):
+        present = jnp.where(sub == s, active_ref[s], present)
+    mask = jnp.where(ply < present, 1.0, 0.0)
+    upper = jnp.where((ply + 1 < present) & (ply + 1 < plies), 0.5, 0.0)
     cos_square = cosine_ref[...]
     terms = jnp.concatenate(
         [
@@ -239,7 +253,7 @@
         axis=0,
     )
     high, low = split_two(terms)
-    only = spread_ref[0, HALF : HALF + LANES, :]
+    only = indicator(ply_spread(plies, width, side)[2])
     spread_terms = jnp.dot(high, only, preferred_element_type=F32) + jnp.dot(
         low, only, preferred_element_type=F32
     )
@@ -268,7 +282,7 @@
             face_x[x + 1, :, cut[t]] = 0.5 * (here[t] * fiber + there[t] * fiber)
         return carry
 
-    lax.fori_loop(0, cells_x - 1, faces_x, 0)
+    lax.fori_loop(0, cells_x - 1, faces_x, 0, unroll=5)
 
     def coefficients(x, carry):
         k = plane(knock, x)
@@ -300,82 +314,68 @@
             along_y[x, :, cut[t]] = ay[t]
             for c in range(cases):
                 value = src[t, pl.ds(c * subs * cells_x + x, subs, stride=cells_x), :]
-                field[c, x, :, cut[t]] = ply_ref[2, :, cut[t]] * value
+                planes[6 + c, x, :, cut[t]] = ply_ref[2, :, cut[t]] * value
         return carry
 
-    lax.fori_loop(0, cells_x, coefficients, 0)
-    copies = [
-        pltpu.make_async_copy(planes, planes_hbm, sems.at[1]),
-        pltpu.make_async_copy(field, field_hbm, sems.at[2]),
-    ]
-    for copy in copies:
-        copy.start()
     for e, x in enumerate((0, cells_x - 1)):
         k = plane(knock, x)
         for t in range(tiles):
-            edge_x[e, :, cut[t]] = k[t] * ply_ref[0, :, cut[t]]
-    for copy in [turned_copy] + copies:
+            planes[1 + e, cells_x, :, cut[t]] = k[t] * ply_ref[0, :, cut[t]]
+    bands = sems.shape[0]
+    band = cells_x // bands
+    copies = []
+    for i in range(bands):
+        lax.fori_loop(i * band, (i + 1) * band, coefficients, 0, unroll=True)
+        part = pl.ds(i * band, band + (1 if i == bands - 1 else 0))
+        copies.append(
+            pltpu.make_async_copy(planes.at[:, part], planes_hbm.at[:, part], sems.at[i])
+        )
+        copies[i].start()
+    for copy in copies:
         copy.wait()
 
 
-def prepare(source, knockdown, orient, active, slot_index, slots):
+def prepare(source, knockdown, orient, active):
     cases, subs, cells_x, width = source.shape
     plies = orient.shape[1]
     side = width // plies
-    rows = slot_index.shape[0]
     cosine = jnp.cos(orient.astype(F32) * (math.pi / 6.0)) ** 2
-    cosine = jnp.pad(cosine, ((0, 0), (0, LANES - plies)))
-    slot_turned = slot_index.reshape(subs, rows // subs).T.reshape(rows)
-    planes = (6, cells_x + 1, subs, width)
-    field = (cases, cells_x, subs, width)
+    planes = (6 + cases, cells_x + 1, subs, width)
     vm = pl.BlockSpec(memory_space=pltpu.VMEM)
-    hbm = pl.BlockSpec(memory_space=pltpu.HBM)
-    shapes = [
-        (planes, F32),
-        (field, F32),
-        ((slots, rows), BF16),
-        ((2, subs, width), F32),
-        ((rows, slots), BF16),
-        ((3, 2 * LANES + HALF, width), BF16),
-        ((width, LANES), BF16),
-        ((width, 2 * LANES), BF16),
-    ]
     return pl.pallas_call(
         functools.partial(prepare_kernel, plies=plies, side=side),
-        out_shape=[jax.ShapeDtypeStruct(*shape) for shape in shapes],
-        in_specs=[vm] * 6,
-        out_specs=[hbm] * 3 + [vm] * 5,
+        out_shape=jax.ShapeDtypeStruct(planes, F32),
+        in_specs=[pl.BlockSpec(memory_space=pltpu.SMEM)] + [vm] * 3,
+        out_specs=pl.BlockSpec(memory_space=pltpu.HBM),
         scratch_shapes=[
             pltpu.VMEM(planes, F32),
-            pltpu.VMEM(field, F32),
-            pltpu.VMEM((slots, rows), BF16),
             pltpu.VMEM((width // LANES, cases * subs * cells_x, LANES), F32),
             pltpu.VMEM((width // LANES, subs * cells_x, LANES), F32),
             pltpu.VMEM((4, subs, width), F32),
-            pltpu.SemaphoreType.DMA((3,)),
-        ],
+            pltpu.SemaphoreType.DMA((4,)),
+        ],
+        compiler_params=pltpu.CompilerParams(vmem_limit_bytes=58 << 20),
         cost_estimate=pl.CostEstimate(
             flops=40_000_000, bytes_accessed=12_000_000, transcendentals=0
         ),
         name="prepare",
-    )(source, knockdown, cosine, active[:, None], slot_turned[:, None], slot_turned[None, :])
+    )(active, source, knockdown, cosine)
 
 
 def solve_kernel(
-    packed_ref, planes_hbm, field_hbm, turned_hit_hbm, edge_x, hit_ref, spread_ref, fold_ref,
-    fold_y_ref, total_hbm, out_ref,
-    planes, field, turned_hit_ref, total, slots, bound, work, resid, side_y, side_x, sems,
+    packed_ref, planes_hbm, slot_ref, slot_row_ref, total_hbm, out_ref,
+    planes, total, slots, hit, bound, work, resid, side_y, side_x, tall, sems,
     *, peers, slot_depth, side,
 ):
+    cases, cells_x, subs, width = total.shape
+    parts = [slice(4, 6 + cases), slice(1, 3), slice(0, 1), slice(3, 4)]
     copies = [
-        pltpu.make_async_copy(field_hbm, field, sems.at[0]),
-        pltpu.make_async_copy(planes_hbm, planes, sems.at[1]),
-        pltpu.make_async_copy(turned_hit_hbm, turned_hit_ref, sems.at[2]),
+        pltpu.make_async_copy(planes_hbm.at[part], planes.at[part], sems.at[k])
+        for k, part in enumerate(parts)
     ]
     for copy in copies:
         copy.start()
     face_x, face_y, face_p, diag, inverse, along_y = (planes.at[k] for k in range(6))
-    cases, cells_x, subs, width = field.shape
     tiles = width // LANES
     lane = lax.broadcasted_iota(jnp.int32, (subs, LANES), 1)
     y_place = lane % side
@@ -391,30 +391,44 @@
 
     unpack_slots(packed_ref, slots, peers, slot_depth)
     pieces = jnp.concatenate(split_two(slots[...]), axis=1)
-    bound[...] = jnp.dot(hit_ref[...], pieces, preferred_element_type=F32).astype(BF16)
-
+    slot_lane = lax.broadcasted_iota(jnp.int32, (subs, peers * slot_depth), 1)
+    for pair in range(2 * side):
+        both = [
+            jnp.where(slot_lane == slot_ref[:, q : q + 1], 1.0, 0.0)
+            for q in (2 * pair, 2 * pair + 1)
+        ]
+        hit[pair * 2 * subs : (pair + 1) * 2 * subs, :] = jnp.concatenate(both, axis=0).astype(BF16)
+    found = jnp.dot(hit[...], pieces, preferred_element_type=F32)
     rows = side * subs
+    lower = lax.broadcasted_iota(jnp.int32, (4 * rows, LANES), 1) < HALF
+    high, low = found[:, :LANES], found[:, LANES:]
+    bound[0] = jnp.where(lower, high, pltpu.roll(low, HALF, 1)).astype(BF16)
+    bound[1] = jnp.where(lower, pltpu.roll(high, HALF, 1), low).astype(BF16)
+
+    ends_x = jnp.concatenate([bound[c, : 2 * rows, :] for c in range(cases)], axis=0)
+    ends_y = jnp.concatenate(
+        [
+            jnp.concatenate([bound[c, 2 * rows : 3 * rows, :], bound[c, 3 * rows :, :]], axis=1)
+            for c in range(cases)
+        ],
+        axis=0,
+    )
+    spread_x = indicator(ply_spread(LANES, width, side)[2])
+    row, y_cell, own = ply_spread(2 * LANES, width, side)
+    spread_y = indicator(own & (y_cell == jnp.where(row < LANES, 0, side - 1)))
+    spread = jnp.dot(ends_x, spread_x, preferred_element_type=F32)
+    side_y[...] = jnp.dot(ends_y, spread_y, preferred_element_type=F32)
     for c in range(cases):
-        own = slice((1 - c) * HALF, (1 - c) * HALF + 2 * LANES)
         for e in range(2):
-            spread = jnp.dot(
-                bound[e * rows : (e + 1) * rows, :],
-                spread_ref[0, own, :],
-                preferred_element_type=F32,
-            )
+            base = (2 * c + e) * rows
             for t in range(tiles):
-                gathered = spread[0:subs, cut[t]]
+                gathered = spread[base : base + subs, cut[t]]
                 for q in range(1, side):
-                    part = spread[q * subs : (q + 1) * subs, cut[t]]
+                    part = spread[base + q * subs : base + (q + 1) * subs, cut[t]]
                     gathered = jnp.where(y_place == q, part, gathered)
                 side_x[c, e, :, cut[t]] = gathered
-        side_y[c] = jnp.dot(
-            bound[2 * rows : 3 * rows, :], spread_ref[1, own, :], preferred_element_type=F32
-        ) + jnp.dot(
-            bound[3 * rows : 4 * rows, :], spread_ref[2, own, :], preferred_element_type=F32
-        )
-    for copy in copies[:2]:
-        copy.wait()
+    copies[0].wait()
+    copies[1].wait()
 
     def residual(x, carry):
         at_first = jnp.where(x == 0, 1.0, 0.0)
@@ -423,16 +437,18 @@
         for c in range(cases):
             for t in range(tiles):
                 value = (
-                    field[c, x, :, cut[t]]
-                    + along_y[x, :, cut[t]] * side_y[c, pl.ds(row, subs), cut[t]]
-                    + at_first * (edge_x[0, :, cut[t]] * side_x[c, 0, :, cut[t]])
-                    + at_final * (edge_x[1, :, cut[t]] * side_x[c, 1, :, cut[t]])
+                    planes[6 + c, x, :, cut[t]]
+                    + along_y[x, :, cut[t]] * side_y[pl.ds(c * rows + row, subs), cut[t]]
+                    + at_first * (planes[1, cells_x, :, cut[t]] * side_x[c, 0, :, cut[t]])
+                    + at_final * (planes[2, cells_x, :, cut[t]] * side_x[c, 1, :, cut[t]])
                 )
                 resid[c, x, :, cut[t]] = value
                 work[0, c, x + 1, :, cut[t]] = (value * inverse[x, :, cut[t]]) * (1.0 / CHEB_CENTER)
         return carry
 
     lax.fori_loop(0, cells_x, residual, 0, unroll=4)
+    copies[2].wait()
+    copies[3].wait()
 
     def operate(x, c, old):
         w = [work[old, c, x + 1, :, cut[t]] for t in range(tiles)]
@@ -476,8 +492,8 @@
                         work[1, c, x + 1, :, cut[t]] = later
                     else:
                         row = pl.multiple_of(x * subs, subs)
-                        side_y[c, pl.ds(row, subs), cut[t]] = along_y[x, :, cut[t]] * (
-                            side_y[c, pl.ds(row, subs), cut[t]] - sums
+                        side_y[pl.ds(c * rows + row, subs), cut[t]] = along_y[x, :, cut[t]] * (
+                            side_y[pl.ds(c * rows + row, subs), cut[t]] - sums
                         )
             return carry
 
@@ -496,40 +512,53 @@
 
         lax.fori_loop(0, cells_x, first, 0, unroll=True)
 
-    total_copy = pltpu.make_async_copy(total, total_hbm, sems.at[3])
+    total_copy = pltpu.make_async_copy(total, total_hbm, sems.at[4])
     total_copy.start()
 
     y_wide = lax.broadcasted_iota(jnp.int32, (subs, width), 1) % side
-    lower = lax.broadcasted_iota(jnp.int32, (rows, LANES), 1) < HALF
+    for c in range(cases):
+        for e, x in enumerate((0, cells_x - 1)):
+            at_ply = planes[1 + e, cells_x] * (side_x[c, e] - total[c, x])
+            for k, piece in enumerate(split_two(at_ply)):
+                wide = piece.astype(F32)
+                at = ((2 * c + e) * 2 + k) * rows
+                tall[at : at + rows, :] = jnp.concatenate(
+                    [jnp.where(y_wide == q, wide, 0.0) for q in range(side)], axis=0
+                ).astype(BF16)
+    across_lanes = (((1,), (1,)), ((), ()))
+    folded_x = lax.dot_general(tall[...], spread_x, across_lanes, preferred_element_type=F32)
+    folded_y = lax.dot_general(
+        jnp.concatenate(split_two(side_y[...]), axis=0),
+        spread_y,
+        across_lanes,
+        preferred_element_type=F32,
+    )
+    folded_y = folded_y[: cases * rows] + folded_y[cases * rows :]
     sums = []
     for c in range(cases):
-        sums_y = jnp.zeros((rows, 2 * LANES), F32)
-        for piece in split_two(side_y[c]):
-            sums_y = sums_y + jnp.dot(piece, fold_y_ref[...], preferred_element_type=F32)
-        sums_x = []
-        for e, x in enumerate((0, cells_x - 1)):
-            at_ply = edge_x[e] * (side_x[c, e] - total[c, x])
-            folded = jnp.zeros((rows, LANES), F32)
-            for piece in split_two(at_ply):
-                wide = piece.astype(F32)
-                tall = jnp.concatenate(
-                    [jnp.where(y_wide == q, wide, 0.0) for q in range(side)], axis=0
-                ).astype(BF16)
-                folded = folded + jnp.dot(tall, fold_ref[...], preferred_element_type=F32)
-            sums_x.append(folded)
-        sums.append(sums_x + [sums_y[:, :LANES], sums_y[:, LANES:]])
-    for e in range(4):
-        both = jnp.where(lower, sums[0][e], pltpu.roll(sums[1][e], HALF, 1))
-        bound[e * rows : (e + 1) * rows, :] = jnp.concatenate(split_two(both), axis=1)
-    copies[2].wait()
-    posted = jnp.dot(turned_hit_ref[...], bound[...], preferred_element_type=F32)
+        own = [
+            folded_x[4 * c * rows + 2 * e * rows : 4 * c * rows + (2 * e + 1) * rows]
+            + folded_x[4 * c * rows + (2 * e + 1) * rows : 4 * c * rows + (2 * e + 2) * rows]
+            for e in range(2)
+        ]
+        part = folded_y[c * rows : (c + 1) * rows]
+        sums.append(own + [part[:, :LANES], part[:, LANES:]])
+    both = [jnp.where(lower[:rows], sums[0][e], sums[1][e]) for e in range(4)]
+    forces = jnp.concatenate(
+        [jnp.concatenate(split_two(part), axis=1) for part in both], axis=0
+    )
+    turned_hit = indicator(
+        lax.broadcasted_iota(jnp.int32, (peers * slot_depth, 4 * rows), 0) == slot_row_ref[...]
+    )
+    posted = jnp.dot(turned_hit, forces, preferred_element_type=F32)
     slots[...] = posted[:, :LANES] + posted[:, LANES:]
     pack_slots(slots, out_ref, peers, slot_depth)
     total_copy.wait()
 
 
-def solve_block(packed, ready, peers, slot_depth, side):
-    cases, cells_x, subs, width = ready[1].shape
+def solve_block(packed, ready, slot_index, source, peers, slot_depth, side):
+    cases, subs, cells_x, width = source.shape
+    points = slot_index.shape[1]
     vm = pl.BlockSpec(memory_space=pltpu.VMEM)
     hbm = pl.BlockSpec(memory_space=pltpu.HBM)
     out_rows = peers * packed_rows(slot_depth)
@@ -540,23 +569,24 @@
             jax.ShapeDtypeStruct((cases,) + planes, F32),
             jax.ShapeDtypeStruct((out_rows, LANES), F32),
         ),
-        in_specs=[vm] + [hbm] * 3 + [vm] * 5,
+        in_specs=[vm, hbm, vm, vm],
         out_specs=(hbm, vm),
         scratch_shapes=[
-            pltpu.VMEM(ready[0].shape, F32),
-            pltpu.VMEM(ready[1].shape, F32),
-            pltpu.VMEM(ready[2].shape, BF16),
+            pltpu.VMEM(ready.shape, F32),
             pltpu.VMEM((cases,) + planes, F32),
             pltpu.VMEM((peers * slot_depth, LANES), F32),
-            pltpu.VMEM((4 * side * subs, 2 * LANES), BF16),
+            pltpu.VMEM((points * subs, peers * slot_depth), BF16),
+            pltpu.VMEM((cases, 4 * side * subs, LANES), BF16),
             pltpu.VMEM((2, cases, cells_x + 2, subs, width), F32),
             pltpu.VMEM((cases,) + planes, F32),
-            pltpu.VMEM((cases, cells_x * subs, width), F32),
+            pltpu.VMEM((cases * side * subs, width), F32),
             pltpu.VMEM((cases, 2, subs, width), F32),
-            pltpu.SemaphoreType.DMA((4,)),
-        ],
+            pltpu.VMEM((4 * cases * side * subs, width), BF16),
+            pltpu.SemaphoreType.DMA((5,)),
+        ],
+        compiler_params=pltpu.CompilerParams(vmem_limit_bytes=51 << 20),
         name="solve_block",
-    )(packed, *ready)
+    )(packed, ready, slot_index, slot_index.T.reshape(1, points * subs))
 
 
 def per_device(shell_state, source, knockdown, orient, active, point_owner, owner_nodes):
@@ -577,18 +607,20 @@
     owners = point_owner.reshape(-1)
     place = jnp.arange(owners.shape[0])
     earlier = (owners[:, None] == owners[None, :]) & (place[None, :] < place[:, None])
-    slot_index = owners * slot_depth + jnp.sum(earlier.astype(jnp.int32), axis=1)
-    ready = prepare(source, knockdown, orient, active, slot_index, peers * slot_depth)
-
+    rank = jnp.sum(earlier.astype(jnp.int32), axis=1).reshape(point_owner.shape)
+    slot_index = point_owner * slot_depth + rank
+    ready = prepare(source, knockdown, orient, active)
     planes, outbound = solve_block(
-        arrived.reshape(peers * per_peer, LANES), ready, peers, slot_depth, side
+        arrived.reshape(peers * per_peer, LANES), ready, slot_index, source, peers, slot_depth, side
     )
     returned = lax.all_to_all(
         outbound.reshape(peers, per_peer, LANES), axes, split_axis=0, concat_axis=0, tiled=True
     )
+    late_nodes, planes = lax.optimization_barrier((nodes, planes))
     adjoint = jnp.transpose(planes, (0, 2, 1, 3))
+    same, late_nodes = pair_slots(late_nodes)
     force = scatter_forces(
-        returned.reshape(peers * per_peer, LANES), nodes, cases * plies, node_local
+        returned.reshape(peers * per_peer, LANES), same, late_nodes, cases * plies, node_local
     )
     return adjoint, force.reshape(cases, plies, node_local)
 

time: 66.4 us -> 57.3 us (0.86)
  Pallas kernels: 33.6 us -> 23.9 us
  waiting for transfers between devices: 12.3 us -> 19.5 us
  local copies, waits for them, and re-layouts: 6.8 us -> 1.61 us
  starting transfers between devices: 12.2 us -> 10.1 us
    all_to_all x1, waiting for transfers between devices: 0.98 us -> 7.8 us  [per_device(): lax.all_to_all(picked.reshape(peers, per_peer, LANES), axes, split_axis=0...]
    pallas_call x1, Pallas kernels: 9.21 us -> 4.46 us  [prepare(): pl.pallas_call(functools.partial(prepare_kernel, plies=plies, side=side),...]
    pallas_call x1, Pallas kernels: 8.45 us -> 4.75 us  [scatter_forces(): pl.pallas_call(functools.partial(scatter_kernel, peers=peers, slot_depth=...]
    unnamed x11 -> x7, local copies, waits for them, and re-layouts: 3.78 us -> 1.13 us
    all_to_all x1, starting transfers between devices: 4.88 us -> 2.79 us  [per_device(): lax.all_to_all(outbound.reshape(peers, per_peer, LANES), axes, split_axis...]
    pallas_call x1, Pallas kernels: 10.2 us -> 8.62 us  [solve_block(): pl.pallas_call(functools.partial(solve_kernel, peers=peers, slot_depth=sl...]
    another operation x2 -> x0, local copies, waits for them, and re-layouts: 1.51 us -> none  [the longest x1 0.82 us: prepare(): slot_turned[:, None]]
    broadcast_in_dim x1 -> x0, local copies, waits for them, and re-layouts: 0.67 us -> none  [prepare(): active[:, None]]
  transfers between devices with their start and end apart: 2 -> 2, of which waited for: 2 -> 2; matrix products, arithmetic and copies ran while one was open for 8% -> 4% of each run, Pallas kernels for 14% -> 9%
where the time goes in v3:
time: 57.3 us; the launch traced here: 56.9 us
  Pallas kernels  23.9 us (42%)
  waiting for transfers between devices  19.5 us (34%)
  starting transfers between devices  10.1 us (18%)
  local copies, waits for them, and re-layouts  1.61 us (3%)
  other arithmetic  0.9 us (2%)
  between operations  0.89 us (2%)
    all_to_all x1, waiting for transfers between devices, per_device(): lax.all_to_all(outbound.reshape(peers, per_peer, LANES), axes, split_axis...  11.7 us
    pallas_call x1, Pallas kernels, solve_block(): pl.pallas_call(functools.partial(solve_kernel, peers=peers, slot_depth=sl...  8.62 us
    all_to_all x1, waiting for transfers between devices, per_device(): lax.all_to_all(picked.reshape(peers, per_peer, LANES), axes, split_axis=0...  7.8 us
    all_to_all x1, starting transfers between devices, per_device(): lax.all_to_all(picked.reshape(peers, per_peer, LANES), axes, split_axis=0...  7.3 us
    pallas_call x1, Pallas kernels, gather_shell(): pl.pallas_call(functools.partial(gather_kernel, peers=peers, slot_depth=s...  5.66 us
    pallas_call x1, Pallas kernels, scatter_forces(): pl.pallas_call(functools.partial(scatter_kernel, peers=peers, slot_depth=...  4.75 us
    pallas_call x1, Pallas kernels, prepare(): pl.pallas_call(functools.partial(prepare_kernel, plies=plies, side=side),...  4.46 us
    all_to_all x1, starting transfers between devices, per_device(): lax.all_to_all(outbound.reshape(peers, per_peer, LANES), axes, split_axis...  2.79 us
  transfers between devices with their start and end apart: 2, of which 2 were waited for; matrix products, arithmetic and copies ran while one was open for 4% of the time, Pallas kernels for 9%

profile of v3, /device:TPU:0, one launch (start us, length us, event | category | flops | bytes accessed | tf_op | source)
XLA Modules:
  0.0 56.9 jit_solution(14159043495247709032)
XLA Ops:
  0.6 0.0 copy-start.1
  0.6 0.0 copy-start.2
  0.7 5.7 %gather_shell.1 = f32[768,128]{1,0:T(8,128)} custom-call(s32[32,32]{1,0:T(8,128)} %bitcast.13, f32[96,8192]{1,0:T(8,128)} %bitcast.18), custom_call_target="tpu_custom_call" | custom-call | tf_op jit(solution)/shard_map/gather_shell/pallas_call | solution.py:94
  6.3 7.3 %all-to-all-start = ((f32[32,24,128]{2,1,0:T(8,128)}), f32[32,24,128]{2,1,0:T(8,128)S(1)}, u32[]{:S(2)}, u32[]{:S(2)}) async-start(f32[32,24,128]{2,1,0:T(8,128)} %bitcast.20), calls=%async_computation | async-start | bytes 786432 | tf_op jit(solution)/shard_map/all_to_all | solution.py:603
  13.6 0.0 copy-done.1
  13.6 0.1 eq.15
  13.7 0.3 convert_reduce_fusion
  14.0 0.1 reshape.40
  14.1 0.1 copy.15
  14.1 0.1 reshape.41.slot_row_ref
  14.2 0.0 copy-done.2
  14.2 0.6 %cosine_multiply_fusion.cosine_ref = f32[8,48]{1,0:T(8,128)} fusion(s32[8,48]{1,0:T(8,128)S(1)} %copy-done.2), kind=kLoop, calls=%fused_computation.4 | loop fusion | flops 1152 | bytes 3072 | tf_op jit(solution)/shard_map/integer_pow | solution.py:342
  14.9 4.5 %prepare.1.planes_hbm = f32[8,17,8,768]{3,2,1,0:T(8,128)} custom-call(s32[8]{0:T(128)} %active_ref.1, bf16[2,8,16,768]{3,2,1,0:T(8,128)(2,1)} %source_ref.1, bf16[8,16,768]{2,1,0:T(8,128)(2,1)} %knock_ref.1, f32[8,48]{1,0:T(8,128)} %cosine_multiply_fusion.cosine_ref), custom_call_target="tpu_custom_call" | custom-call | flops 40000000 | bytes 12000000 | tf_op jit(solution)/shard_map/prepare/pallas_call | solution.py:345
  19.4 0.0 copy-start
  19.4 7.8 %all-to-all-done = f32[32,24,128]{2,1,0:T(8,128)S(1)} async-done(((f32[32,24,128]{2,1,0:T(8,128)}), f32[32,24,128]{2,1,0:T(8,128)S(1)}, u32[]{:S(2)}, u32[]{:S(2)}) %all-to-all-start) | async-done | bytes 393248 | tf_op jit(solution)/shard_map/all_to_all | solution.py:603
  27.2 8.6 %solve_block.1 = (f32[2,16,8,768]{3,2,1,0:T(8,128)S(1)}, f32[768,128]{1,0:T(8,128)}) custom-call(f32[768,128]{1,0:T(8,128)S(1)} %bitcast.10, f32[8,17,8,768]{3,2,1,0:T(8,128)} %prepare.1.planes_hbm, s32[8,64]{1,0:T(8,128)S(1)} %multiply_add_fusion.slot_ref, s32[1,512]{1,0:T(1,128)S(1)} %reshape.41.slot_row_ref), custom_call_target="tpu_custom_call" | custom-call | tf_op jit(solution)/shard_map/solve_block/pallas_call | solution.py:566
  35.8 2.8 %all-to-all-start.1 = ((f32[32,24,128]{2,1,0:T(8,128)}), f32[32,24,128]{2,1,0:T(8,128)S(1)}, u32[]{:S(2)}, u32[]{:S(2)}) async-start(f32[32,24,128]{2,1,0:T(8,128)} %bitcast.7), calls=%async_computation.1 | async-start | bytes 786432 | tf_op jit(solution)/shard_map/all_to_all | solution.py:616
  38.6 1.1 %copy.17 = f32[2,8,16,768]{3,2,1,0:T(8,128)} copy(f32[2,8,16,768]{3,1,2,0:T(8,128)S(1)} %bitcast.12) | data formatting | bytes 1572864
  39.7 0.0 copy-done
  39.7 0.1 reshape.42.node_row_ref
  39.8 0.1 copy.16.node_turned_ref
  39.9 0.4 pair_slots.1
  40.3 11.7 %all-to-all-done.1 = f32[32,24,128]{2,1,0:T(8,128)S(1)} async-done(((f32[32,24,128]{2,1,0:T(8,128)}), f32[32,24,128]{2,1,0:T(8,128)S(1)}, u32[]{:S(2)}, u32[]{:S(2)}) %all-to-all-start.1) | async-done | bytes 393248 | tf_op jit(solution)/shard_map/all_to_all | solution.py:616
  52.0 4.7 %scatter_forces.1 = f32[96,8192]{1,0:T(8,128)} custom-call(s32[32,32]{1,0:T(8,128)S(1)} %get-tuple-element.11.node_ref, bf16[1024,1024]{1,0:T(8,128)(2,1)S(1)} %get-tuple-element.12.same_ref, f32[768,128]{1,0:T(8,128)S(1)} %bitcast.11), custom_call_target="tpu_custom_call" | custom-call | tf_op jit(solution)/shard_map/scatter_forces/pallas_call | solution.py:181
  (1 shorter events, 0.0 us)
Async XLA Ops:
  0.6 13.0 %copy-start.1 = (s32[8,64]{1,0:T(8,128)S(1)}, s32[8,64]{1,0:T(8,128)}, u32[]{:S(2)}) copy-start(s32[8,64]{1,0:T(8,128)} %param.12) | copy-start | bytes 6148
  0.6 13.6 %copy-start.2 = (s32[8,48]{1,0:T(8,128)S(1)}, s32[8,48]{1,0:T(8,128)}, u32[]{:S(2)}) copy-start(s32[8,48]{1,0:T(8,128)} %param.10) | copy-start | bytes 4612
  6.3 20.9 %all-to-all-start = ((f32[32,24,128]{2,1,0:T(8,128)}), f32[32,24,128]{2,1,0:T(8,128)S(1)}, u32[]{:S(2)}, u32[]{:S(2)}) async-start(f32[32,24,128]{2,1,0:T(8,128)} %bitcast.20), calls=%async_computation | async-start | bytes 786432 | tf_op jit(solution)/shard_map/all_to_all | solution.py:603
  19.4 20.4 %copy-start = (s32[1,32,32]{2,1,0:T(8,128)S(1)}, s32[1,32,32]{2,1,0:T(8,128)}, u32[]{:S(2)}) copy-start(s32[1,32,32]{2,1,0:T(8,128)} %param.13) | copy-start | bytes 12292
  35.8 16.2 %all-to-all-start.1 = ((f32[32,24,128]{2,1,0:T(8,128)}), f32[32,24,128]{2,1,0:T(8,128)S(1)}, u32[]{:S(2)}, u32[]{:S(2)}) async-start(f32[32,24,128]{2,1,0:T(8,128)} %bitcast.7), calls=%async_computation.1 | async-start | bytes 786432 | tf_op jit(solution)/shard_map/all_to_all | solution.py:616

commit v4 on v3

--- a/solution.py
+++ b/solution.py
@@ -82,7 +82,7 @@
             rows[pl.ds(slot, 1), :] = turned[pl.ds(node_ref[peer, u] + 8, 1), :]
         return carry
 
-    lax.fori_loop(0, peers, pick, 0)
+    lax.fori_loop(0, peers, pick, 0, unroll=4)
     pack_slots(rows, out_ref, peers, slot_depth)
 
 
@@ -157,7 +157,7 @@
             total[pl.ds(node_ref[peer, u] + 8, 1), :] = rows[pl.ds(slot, 1), :]
         return carry
 
-    lax.fori_loop(0, peers, put, 0)
+    lax.fori_loop(0, peers, put, 0, unroll=4)
 
     chunks = sems.shape[0]
     chunk = node_local // chunks
@@ -199,22 +199,22 @@
     return high, (value - high.astype(F32)).astype(BF16)
 
 
-def from_lower_ply(values, low_ply, side):
-    turned = [pltpu.roll(v, side, 1) for v in values]
-    return [jnp.where(low_ply, turned[t - 1], turned[t]) for t in range(len(values))]
-
-
-def from_upper_ply(values, high_ply, side):
-    turned = [pltpu.roll(v, LANES - side, 1) for v in values]
-    return [
-        jnp.where(high_ply, turned[t + 1], turned[t]) for t in range(len(values) - 1)
-    ] + [turned[-1]]
+def ply_of(cell, width, side):
+    return cell % LANES // side * (width // LANES) + cell // LANES
+
+
+def from_lower_ply(values, side):
+    return [pltpu.roll(values[-1], side, 1)] + values[:-1]
+
+
+def from_upper_ply(values, side):
+    return values[1:] + [pltpu.roll(values[0], LANES - side, 1)]
 
 
 def ply_spread(tall, width, side):
     row = lax.broadcasted_iota(jnp.int32, (tall, width), 0)
     cell = lax.broadcasted_iota(jnp.int32, (tall, width), 1)
-    return row, cell % side, row % HALF == cell // side
+    return row, cell % side, row % HALF == ply_of(cell, width, side)
 
 
 def indicator(condition):
@@ -231,8 +231,6 @@
     y_place = lane % side
     first_y = y_place == 0
     last_y = y_place == side - 1
-    low_ply = lane < side
-    high_ply = lane >= LANES - side
     cut = [slice(t * LANES, (t + 1) * LANES) for t in range(tiles)]
 
     ply = lax.broadcasted_iota(jnp.int32, (subs, plies), 1)
@@ -260,12 +258,13 @@
     for k in range(4):
         ply_ref[k] = spread_terms[k * subs : (k + 1) * subs, :]
 
-    for s in range(subs):
+    natural = lax.broadcasted_iota(jnp.int32, (width, width), 0)
+    cell = lax.broadcasted_iota(jnp.int32, (width, width), 1)
+    order = indicator(natural == ply_of(cell, width, side) * side + cell % side)
+    for ref, into in ((source_ref, src), (knock_ref, knock)):
+        ordered = jnp.dot(ref[...].reshape(-1, width), order, preferred_element_type=F32)
         for t in range(tiles):
-            knock[t, s * cells_x : (s + 1) * cells_x, :] = knock_ref[s, :, cut[t]].astype(F32)
-            for c in range(cases):
-                at = (c * subs + s) * cells_x
-                src[t, at : at + cells_x, :] = source_ref[c, s, :, cut[t]].astype(F32)
+            into[t] = ordered[:, cut[t]]
 
     def plane(ref, x, base=0):
         return [ref[t, pl.ds(base + x, subs, stride=cells_x), :] for t in range(tiles)]
@@ -289,9 +288,9 @@
         ax = [k[t] * ply_ref[0, :, cut[t]] for t in range(tiles)]
         ay = [k[t] * ply_ref[1, :, cut[t]] for t in range(tiles)]
         ac = [k[t] * (THROUGH * ply_ref[2, :, cut[t]]) for t in range(tiles)]
-        up = from_upper_ply(ac, high_ply, side)
+        up = from_upper_ply(ac, side)
         fp = [ply_ref[3, :, cut[t]] * (ac[t] + up[t]) for t in range(tiles)]
-        below = from_lower_ply(fp, low_ply, side)
+        below = from_lower_ply(fp, side)
         at_edge = jnp.where((x == 0) | (x == cells_x - 1), 1.0, 0.0)
         for t in range(tiles):
             fy = jnp.where(last_y, 0.0, 0.5 * (ay[t] + pltpu.roll(ay[t], LANES - 1, 1)))
@@ -363,8 +362,8 @@
 
 
 def solve_kernel(
-    packed_ref, planes_hbm, slot_ref, slot_row_ref, total_hbm, out_ref,
-    planes, total, slots, hit, bound, work, resid, side_y, side_x, tall, sems,
+    packed_ref, planes_hbm, slot_ref, slot_row_ref, total, out_ref,
+    planes, slots, hit, bound, work, resid, side_y, side_x, tall, sems,
     *, peers, slot_depth, side,
 ):
     cases, cells_x, subs, width = total.shape
@@ -379,8 +378,6 @@
     tiles = width // LANES
     lane = lax.broadcasted_iota(jnp.int32, (subs, LANES), 1)
     y_place = lane % side
-    low_ply = lane < side
-    high_ply = lane >= LANES - side
     cut = [slice(t * LANES, (t + 1) * LANES) for t in range(tiles)]
 
     zero = jnp.zeros((subs, width), F32)
@@ -453,8 +450,8 @@
     def operate(x, c, old):
         w = [work[old, c, x + 1, :, cut[t]] for t in range(tiles)]
         fp = [face_p[x, :, cut[t]] for t in range(tiles)]
-        below = from_lower_ply([fp[t] * w[t] for t in range(tiles)], low_ply, side)
-        above = from_upper_ply(w, high_ply, side)
+        below = from_lower_ply([fp[t] * w[t] for t in range(tiles)], side)
+        above = from_upper_ply(w, side)
         out = []
         for t in range(tiles):
             fy = face_y[x, :, cut[t]]
@@ -512,9 +509,6 @@
 
         lax.fori_loop(0, cells_x, first, 0, unroll=True)
 
-    total_copy = pltpu.make_async_copy(total, total_hbm, sems.at[4])
-    total_copy.start()
-
     y_wide = lax.broadcasted_iota(jnp.int32, (subs, width), 1) % side
     for c in range(cases):
         for e, x in enumerate((0, cells_x - 1)):
@@ -553,7 +547,6 @@
     posted = jnp.dot(turned_hit, forces, preferred_element_type=F32)
     slots[...] = posted[:, :LANES] + posted[:, LANES:]
     pack_slots(slots, out_ref, peers, slot_depth)
-    total_copy.wait()
 
 
 def solve_block(packed, ready, slot_index, source, peers, slot_depth, side):
@@ -570,10 +563,9 @@
             jax.ShapeDtypeStruct((out_rows, LANES), F32),
         ),
         in_specs=[vm, hbm, vm, vm],
-        out_specs=(hbm, vm),
+        out_specs=(vm, vm),
         scratch_shapes=[
             pltpu.VMEM(ready.shape, F32),
-            pltpu.VMEM((cases,) + planes, F32),
             pltpu.VMEM((peers * slot_depth, LANES), F32),
             pltpu.VMEM((points * subs, peers * slot_depth), BF16),
             pltpu.VMEM((cases, 4 * side * subs, LANES), BF16),
@@ -582,11 +574,55 @@
             pltpu.VMEM((cases * side * subs, width), F32),
             pltpu.VMEM((cases, 2, subs, width), F32),
             pltpu.VMEM((4 * cases * side * subs, width), BF16),
-            pltpu.SemaphoreType.DMA((5,)),
+            pltpu.SemaphoreType.DMA((4,)),
         ],
         compiler_params=pltpu.CompilerParams(vmem_limit_bytes=51 << 20),
         name="solve_block",
     )(packed, ready, slot_index, slot_index.T.reshape(1, points * subs))
+
+
+def finish_kernel(total_ref, adjoint_ref, turned, *, side):
+    cases, cells_x, subs, width = total_ref.shape
+    rows = cases * cells_x * subs
+    value = total_ref[...].reshape(rows, width)
+    high = value.astype(BF16)
+    rest = value - high.astype(F32)
+    middle, low = split_two(rest)
+    cell = lax.broadcasted_iota(jnp.int32, (width, width), 0)
+    natural = lax.broadcasted_iota(jnp.int32, (width, width), 1)
+    order = indicator(natural == ply_of(cell, width, side) * side + cell % side)
+    found = jnp.dot(
+        jnp.concatenate([high, middle, low], axis=0), order, preferred_element_type=F32
+    )
+    found = (found[:rows] + found[rows : 2 * rows]) + found[2 * rows :]
+    for t in range(width // LANES):
+        cut = slice(t * LANES, (t + 1) * LANES)
+        for c in range(cases):
+            for x in range(cells_x):
+                at = (c * cells_x + x) * subs
+                turned[t, pl.ds(c * subs * cells_x + x, subs, stride=cells_x), :] = found[
+                    at : at + subs, cut
+                ]
+        adjoint_ref[:, cut] = turned[t]
+
+
+def finish(total, side):
+    cases, cells_x, subs, width = total.shape
+    rows = cases * cells_x * subs
+    vm = pl.BlockSpec(memory_space=pltpu.VMEM)
+    adjoint = pl.pallas_call(
+        functools.partial(finish_kernel, side=side),
+        out_shape=jax.ShapeDtypeStruct((rows, width), F32),
+        in_specs=[vm],
+        out_specs=vm,
+        scratch_shapes=[pltpu.VMEM((width // LANES, rows, LANES), F32)],
+        compiler_params=pltpu.CompilerParams(vmem_limit_bytes=24 << 20),
+        cost_estimate=pl.CostEstimate(
+            flops=10_000_000, bytes_accessed=8_000_000, transcendentals=0
+        ),
+        name="finish",
+    )(total)
+    return adjoint.reshape(cases, subs, cells_x, width)
 
 
 def per_device(shell_state, source, knockdown, orient, active, point_owner, owner_nodes):
@@ -617,7 +653,7 @@
         outbound.reshape(peers, per_peer, LANES), axes, split_axis=0, concat_axis=0, tiled=True
     )
     late_nodes, planes = lax.optimization_barrier((nodes, planes))
-    adjoint = jnp.transpose(planes, (0, 2, 1, 3))
+    adjoint = finish(planes, side)
     same, late_nodes = pair_slots(late_nodes)
     force = scatter_forces(
         returned.reshape(peers * per_peer, LANES), same, late_nodes, cases * plies, node_local

time: 57.3 us -> 55.2 us (0.963)
  local copies, waits for them, and re-layouts: 1.61 us -> 0.5 us
  waiting for transfers between devices: 19.5 us -> 18.7 us
    pallas_call x0 -> x1, Pallas kernels: none -> 2.26 us  [finish(): pl.pallas_call(functools.partial(finish_kernel, side=side), out_shape=jax...]
    pallas_call x1, Pallas kernels: 8.62 us -> 6.77 us  [solve_block(): pl.pallas_call(functools.partial(solve_kernel, peers=peers, slot_depth=sl...]
    all_to_all x1, waiting for transfers between devices: 11.7 us -> 10.5 us  [per_device(): lax.all_to_all(outbound.reshape(peers, per_peer, LANES), axes, split_axis...]
    unnamed x7 -> x6, local copies, waits for them, and re-layouts: 1.13 us -> 0.01 us
  transfers between devices with their start and end apart: 2 -> 2, of which waited for: 2 -> 2; matrix products, arithmetic and copies ran while one was open for 4% -> 3% of each run, Pallas kernels for 9% -> 12%
where the time goes in v4:
time: 55.2 us; the launch traced here: 54.8 us
  Pallas kernels  23.7 us (43%)
  waiting for transfers between devices  18.7 us (34%)
  starting transfers between devices  10.1 us (18%)
  other arithmetic  0.9 us (2%)
  between operations  0.89 us (2%)
    all_to_all x1, waiting for transfers between devices, per_device(): lax.all_to_all(outbound.reshape(peers, per_peer, LANES), axes, split_axis...  10.5 us
    all_to_all x1, waiting for transfers between devices, per_device(): lax.all_to_all(picked.reshape(peers, per_peer, LANES), axes, split_axis=0...  8.17 us
    all_to_all x1, starting transfers between devices, per_device(): lax.all_to_all(picked.reshape(peers, per_peer, LANES), axes, split_axis=0...  7.3 us
    pallas_call x1, Pallas kernels, solve_block(): pl.pallas_call(functools.partial(solve_kernel, peers=peers, slot_depth=sl...  6.77 us
    pallas_call x1, Pallas kernels, gather_shell(): pl.pallas_call(functools.partial(gather_kernel, peers=peers, slot_depth=s...  5.53 us
    pallas_call x1, Pallas kernels, scatter_forces(): pl.pallas_call(functools.partial(scatter_kernel, peers=peers, slot_depth=...  4.61 us
    pallas_call x1, Pallas kernels, prepare(): pl.pallas_call(functools.partial(prepare_kernel, plies=plies, side=side),...  4.09 us
    all_to_all x1, starting transfers between devices, per_device(): lax.all_to_all(outbound.reshape(peers, per_peer, LANES), axes, split_axis...  2.79 us
  transfers between devices with their start and end apart: 2, of which 2 were waited for; matrix products, arithmetic and copies ran while one was open for 3% of the time, Pallas kernels for 12%

profile of v4, /device:TPU:0, one launch (start us, length us, event | category | flops | bytes accessed | tf_op | source)
XLA Modules:
  0.0 54.8 jit_solution(4107001353752785321)
XLA Ops:
  0.6 0.0 copy-start.1
  0.6 0.0 copy-start.2
  0.7 5.5 %gather_shell.1 = f32[768,128]{1,0:T(8,128)} custom-call(s32[32,32]{1,0:T(8,128)} %bitcast.12, f32[96,8192]{1,0:T(8,128)} %bitcast.17), custom_call_target="tpu_custom_call" | custom-call | tf_op jit(solution)/shard_map/gather_shell/pallas_call | solution.py:94
  6.2 7.3 %all-to-all-start = ((f32[32,24,128]{2,1,0:T(8,128)}), f32[32,24,128]{2,1,0:T(8,128)S(1)}, u32[]{:S(2)}, u32[]{:S(2)}) async-start(f32[32,24,128]{2,1,0:T(8,128)} %bitcast.19), calls=%async_computation | async-start | bytes 786432 | tf_op jit(solution)/shard_map/all_to_all | solution.py:639
  13.5 0.0 copy-done.1
  13.5 0.1 eq.15
  13.6 0.3 convert_reduce_fusion
  13.8 0.1 reshape.43
  13.9 0.1 copy.13
  14.0 0.1 reshape.44.slot_row_ref
  14.1 0.0 copy-done.2
  14.1 0.6 %cosine_multiply_fusion.cosine_ref = f32[8,48]{1,0:T(8,128)} fusion(s32[8,48]{1,0:T(8,128)S(1)} %copy-done.2), kind=kLoop, calls=%fused_computation.4 | loop fusion | flops 1152 | bytes 3072 | tf_op jit(solution)/shard_map/integer_pow | solution.py:341
  14.8 4.1 %prepare.1.planes_hbm = f32[8,17,8,768]{3,2,1,0:T(8,128)} custom-call(s32[8]{0:T(128)} %active_ref.1, bf16[2,8,16,768]{3,2,1,0:T(8,128)(2,1)} %source_ref.1, bf16[8,16,768]{2,1,0:T(8,128)(2,1)} %knock_ref.1, f32[8,48]{1,0:T(8,128)} %cosine_multiply_fusion.cosine_ref), custom_call_target="tpu_custom_call" | custom-call | flops 40000000 | bytes 12000000 | tf_op jit(solution)/shard_map/prepare/pallas_call | solution.py:344
  18.9 0.0 copy-start
  18.9 8.2 %all-to-all-done = f32[32,24,128]{2,1,0:T(8,128)S(1)} async-done(((f32[32,24,128]{2,1,0:T(8,128)}), f32[32,24,128]{2,1,0:T(8,128)S(1)}, u32[]{:S(2)}, u32[]{:S(2)}) %all-to-all-start) | async-done | bytes 393248 | tf_op jit(solution)/shard_map/all_to_all | solution.py:639
  27.0 6.8 %solve_block.1 = (f32[2,16,8,768]{3,2,1,0:T(8,128)S(1)}, f32[768,128]{1,0:T(8,128)}) custom-call(f32[768,128]{1,0:T(8,128)S(1)} %bitcast.10, f32[8,17,8,768]{3,2,1,0:T(8,128)} %prepare.1.planes_hbm, s32[8,64]{1,0:T(8,128)S(1)} %multiply_add_fusion.slot_ref, s32[1,512]{1,0:T(1,128)S(1)} %reshape.44.slot_row_ref), custom_call_target="tpu_custom_call" | custom-call | tf_op jit(solution)/shard_map/solve_block/pallas_call | solution.py:559
  33.8 2.8 %all-to-all-start.1 = ((f32[32,24,128]{2,1,0:T(8,128)}), f32[32,24,128]{2,1,0:T(8,128)S(1)}, u32[]{:S(2)}, u32[]{:S(2)}) async-start(f32[32,24,128]{2,1,0:T(8,128)} %bitcast.7), calls=%async_computation.1 | async-start | bytes 786432 | tf_op jit(solution)/shard_map/all_to_all | solution.py:652
  36.6 0.0 copy-done
  36.6 0.1 reshape.46.node_row_ref
  36.7 0.1 copy.14.node_turned_ref
  36.8 0.4 pair_slots.1
  37.2 2.3 %finish.1 = f32[256,768]{1,0:T(8,128)} custom-call(f32[2,16,8,768]{3,2,1,0:T(8,128)S(1)} %get-tuple-element.9.total_ref), custom_call_target="tpu_custom_call" | custom-call | flops 10000000 | bytes 8000000 | tf_op jit(solution)/shard_map/finish/pallas_call | solution.py:613
  39.5 10.5 %all-to-all-done.1 = f32[32,24,128]{2,1,0:T(8,128)S(1)} async-done(((f32[32,24,128]{2,1,0:T(8,128)}), f32[32,24,128]{2,1,0:T(8,128)S(1)}, u32[]{:S(2)}, u32[]{:S(2)}) %all-to-all-start.1) | async-done | bytes 393248 | tf_op jit(solution)/shard_map/all_to_all | solution.py:652
  50.0 4.6 %scatter_forces.1 = f32[96,8192]{1,0:T(8,128)} custom-call(s32[32,32]{1,0:T(8,128)S(1)} %get-tuple-element.11.node_ref, bf16[1024,1024]{1,0:T(8,128)(2,1)S(1)} %get-tuple-element.12.same_ref, f32[768,128]{1,0:T(8,128)S(1)} %bitcast.11), custom_call_target="tpu_custom_call" | custom-call | tf_op jit(solution)/shard_map/scatter_forces/pallas_call | solution.py:181
  (1 shorter events, 0.0 us)
Async XLA Ops:
  0.6 12.9 %copy-start.1 = (s32[8,64]{1,0:T(8,128)S(1)}, s32[8,64]{1,0:T(8,128)}, u32[]{:S(2)}) copy-start(s32[8,64]{1,0:T(8,128)} %param.12) | copy-start | bytes 6148
  0.6 13.5 %copy-start.2 = (s32[8,48]{1,0:T(8,128)S(1)}, s32[8,48]{1,0:T(8,128)}, u32[]{:S(2)}) copy-start(s32[8,48]{1,0:T(8,128)} %param.10) | copy-start | bytes 4612
  6.2 20.9 %all-to-all-start = ((f32[32,24,128]{2,1,0:T(8,128)}), f32[32,24,128]{2,1,0:T(8,128)S(1)}, u32[]{:S(2)}, u32[]{:S(2)}) async-start(f32[32,24,128]{2,1,0:T(8,128)} %bitcast.19), calls=%async_computation | async-start | bytes 786432 | tf_op jit(solution)/shard_map/all_to_all | solution.py:639
  18.9 17.8 %copy-start = (s32[1,32,32]{2,1,0:T(8,128)S(1)}, s32[1,32,32]{2,1,0:T(8,128)}, u32[]{:S(2)}) copy-start(s32[1,32,32]{2,1,0:T(8,128)} %param.13) | copy-start | bytes 12292
  33.8 16.2 %all-to-all-start.1 = ((f32[32,24,128]{2,1,0:T(8,128)}), f32[32,24,128]{2,1,0:T(8,128)S(1)}, u32[]{:S(2)}, u32[]{:S(2)}) async-start(f32[32,24,128]{2,1,0:T(8,128)} %bitcast.7), calls=%async_computation.1 | async-start | bytes 786432 | tf_op jit(solution)/shard_map/all_to_all | solution.py:652

commit v5 on v4

--- a/solution.py
+++ b/solution.py
@@ -58,7 +58,18 @@
         rows_ref[g * 32 + 24 : g * 32 + 32, :] = extra
 
 
-def gather_kernel(node_ref, shell_hbm, out_ref, shell, turned, rows, sems, *, peers, slot_depth):
+def split_two(value):
+    high = value.astype(BF16)
+    return high, (value - high.astype(F32)).astype(BF16)
+
+
+def indicator(condition):
+    return jnp.where(condition, 1.0, 0.0).astype(BF16)
+
+
+def gather_kernel(
+    node_ref, shell_hbm, out_hbm, shell, turned, rows, packed, sems, out_sems, *, peers, slot_depth
+):
     width, node_local = shell.shape
     chunks = sems.shape[0]
     chunk = node_local // chunks
@@ -68,9 +79,23 @@
         copies.append(pltpu.make_async_copy(shell_hbm.at[:, part], shell.at[:, part], sems.at[i]))
         copies[i].start()
     gap = jnp.zeros((HALF - width // 2, LANES), F32)
+    gap_two = jnp.zeros((HALF - width // 2, 2 * LANES), F32)
+    unit_row = lax.broadcasted_iota(jnp.int32, (2 * LANES, 2 * LANES), 0)
+    unit = indicator(unit_row == lax.broadcasted_iota(jnp.int32, (2 * LANES, 2 * LANES), 1))
+    across_lanes = (((1,), (1,)), ((), ()))
+    tiles = chunk // LANES
+    in_matmul = tiles // 8 * 2
     for i in range(chunks):
         copies[i].wait()
-        for t in range(i * chunk // LANES, (i + 1) * chunk // LANES):
+        for t in range(i * tiles, i * tiles + in_matmul, 2):
+            tile = shell[:, t * LANES : (t + 2) * LANES]
+            both = jnp.concatenate(
+                [tile[: width // 2], gap_two, tile[width // 2 :], gap_two], axis=0
+            )
+            pieces = jnp.concatenate(split_two(both), axis=0)
+            out = lax.dot_general(unit, pieces, across_lanes, preferred_element_type=F32)
+            turned[8 + t * LANES : 8 + (t + 2) * LANES, :] = out[:, :LANES] + out[:, LANES:]
+        for t in range(i * tiles + in_matmul, (i + 1) * tiles):
             tile = shell[:, t * LANES : (t + 1) * LANES]
             parts = [tile[: width // 2], gap, tile[width // 2 :], gap]
             turned[8 + t * LANES : 8 + (t + 1) * LANES, :] = jnp.concatenate(parts, axis=0).T
@@ -82,14 +107,25 @@
             rows[pl.ds(slot, 1), :] = turned[pl.ds(node_ref[peer, u] + 8, 1), :]
         return carry
 
-    lax.fori_loop(0, peers, pick, 0, unroll=4)
-    pack_slots(rows, out_ref, peers, slot_depth)
+    groups = out_sems.shape[0]
+    share = peers // groups
+    per_peer = packed_rows(slot_depth)
+    sends = []
+    for g in range(groups):
+        lax.fori_loop(g * share, (g + 1) * share, pick, 0, unroll=4)
+        own = slice(g * share * slot_depth, (g + 1) * share * slot_depth)
+        part = slice(g * share * per_peer, (g + 1) * share * per_peer)
+        pack_slots(rows.at[own], packed.at[part], share, slot_depth)
+        sends.append(pltpu.make_async_copy(packed.at[part], out_hbm.at[part], out_sems.at[g]))
+        sends[g].start()
+    for send in sends:
+        send.wait()
 
 
 def gather_shell(shell_flat, nodes):
     width, node_local = shell_flat.shape
     peers, slot_depth = nodes.shape
-    chunks = 8
+    chunks, groups = 4, 8
     out_rows = peers * packed_rows(slot_depth)
     return pl.pallas_call(
         functools.partial(gather_kernel, peers=peers, slot_depth=slot_depth),
@@ -98,20 +134,21 @@
             pl.BlockSpec(memory_space=pltpu.SMEM),
             pl.BlockSpec(memory_space=pltpu.HBM),
         ],
-        out_specs=pl.BlockSpec(memory_space=pltpu.VMEM),
+        out_specs=pl.BlockSpec(memory_space=pltpu.HBM),
         scratch_shapes=[
             pltpu.VMEM((width, node_local), F32),
             pltpu.VMEM((node_local + 8, LANES), F32),
             pltpu.VMEM((peers * slot_depth, LANES), F32),
+            pltpu.VMEM((out_rows, LANES), F32),
             pltpu.SemaphoreType.DMA((chunks,)),
+            pltpu.SemaphoreType.DMA((groups,)),
         ],
         name="gather_shell",
     )(nodes, shell_flat)
 
 
-def pair_kernel(node_turned_ref, node_row_ref, node_ref, same_ref, node_out_ref):
+def pair_kernel(node_turned_ref, node_row_ref, same_ref):
     depth, peers = node_turned_ref.shape
-    node_out_ref[...] = node_ref[...]
     for peer in range(peers):
         column = node_turned_ref[:, peer : peer + 1]
         same_ref[peer * depth : (peer + 1) * depth, :] = jnp.where(
@@ -125,22 +162,19 @@
     vm = pl.BlockSpec(memory_space=pltpu.VMEM)
     return pl.pallas_call(
         pair_kernel,
-        out_shape=[
-            jax.ShapeDtypeStruct((slots, slots), BF16),
-            jax.ShapeDtypeStruct(nodes.shape, jnp.int32),
-        ],
-        in_specs=[vm] * 3,
-        out_specs=[vm] * 2,
+        out_shape=jax.ShapeDtypeStruct((slots, slots), BF16),
+        in_specs=[vm] * 2,
+        out_specs=vm,
         compiler_params=pltpu.CompilerParams(vmem_limit_bytes=16 << 20),
         cost_estimate=pl.CostEstimate(
             flops=4_000_000, bytes_accessed=4_000_000, transcendentals=0
         ),
         name="pair_slots",
-    )(nodes.T, nodes.reshape(1, slots), nodes)
+    )(nodes.T, nodes.reshape(1, slots))
 
 
 def scatter_kernel(
-    node_ref, same_ref, packed_ref, out_hbm, total, rows, out, sems, *, peers, slot_depth
+    row_ref, same_ref, packed_ref, out_hbm, total, rows, out, sems, *, peers, slot_depth
 ):
     width, node_local = out.shape
     unpack_slots(packed_ref, rows, peers, slot_depth)
@@ -151,13 +185,13 @@
     summed = jnp.dot(same_ref[...], pieces, preferred_element_type=F32)
     rows[...] = summed[:, :LANES] + summed[:, LANES:]
 
-    def put(peer, carry):
-        for u in range(slot_depth):
-            slot = peer * slot_depth + u
-            total[pl.ds(node_ref[peer, u] + 8, 1), :] = rows[pl.ds(slot, 1), :]
+    def put(group, carry):
+        for u in range(LANES):
+            slot = group * LANES + u
+            total[pl.ds(row_ref[slot], 1), :] = rows[pl.ds(slot, 1), :]
         return carry
 
-    lax.fori_loop(0, peers, put, 0, unroll=4)
+    lax.fori_loop(0, peers * slot_depth // LANES, put, 0)
 
     chunks = sems.shape[0]
     chunk = node_local // chunks
@@ -174,8 +208,7 @@
         copy.wait()
 
 
-def scatter_forces(packed, same, nodes, width, node_local):
-    peers, slot_depth = nodes.shape
+def scatter_forces(packed, same, node_rows, peers, slot_depth, width, node_local):
     chunks = 8
     vm = pl.BlockSpec(memory_space=pltpu.VMEM)
     return pl.pallas_call(
@@ -191,12 +224,7 @@
         ],
         compiler_params=pltpu.CompilerParams(vmem_limit_bytes=40 << 20),
         name="scatter_forces",
-    )(nodes, same, packed)
-
-
-def split_two(value):
-    high = value.astype(BF16)
-    return high, (value - high.astype(F32)).astype(BF16)
+    )(node_rows, same, packed)
 
 
 def ply_of(cell, width, side):
@@ -215,10 +243,6 @@
     row = lax.broadcasted_iota(jnp.int32, (tall, width), 0)
     cell = lax.broadcasted_iota(jnp.int32, (tall, width), 1)
     return row, cell % side, row % HALF == ply_of(cell, width, side)
-
-
-def indicator(condition):
-    return jnp.where(condition, 1.0, 0.0).astype(BF16)
 
 
 def prepare_kernel(
@@ -654,9 +678,11 @@
     )
     late_nodes, planes = lax.optimization_barrier((nodes, planes))
     adjoint = finish(planes, side)
-    same, late_nodes = pair_slots(late_nodes)
+    same = pair_slots(late_nodes)
+    node_rows = late_nodes.reshape(-1) + 8
     force = scatter_forces(
-        returned.reshape(peers * per_peer, LANES), same, late_nodes, cases * plies, node_local
+        returned.reshape(peers * per_peer, LANES), same, node_rows, peers, slot_depth,
+        cases * plies, node_local,
     )
     return adjoint, force.reshape(cases, plies, node_local)
 

time: 55.2 us -> 54.3 us (0.984)
  Pallas kernels: 23.7 us -> 22.9 us
    pallas_call x1, Pallas kernels: 5.53 us -> 4.89 us  [gather_shell(): pl.pallas_call(functools.partial(gather_kernel, peers=peers, slot_depth=s...]
  transfers between devices with their start and end apart: 2 -> 2, of which waited for: 2 -> 2; matrix products, arithmetic and copies ran while one was open for 3% -> 3% of each run, Pallas kernels for 12% -> 13%
where the time goes in v5:
time: 54.3 us; the launch traced here: 53.9 us
  Pallas kernels  22.9 us (42%)
  waiting for transfers between devices  18.4 us (34%)
  starting transfers between devices  10.1 us (19%)
  other arithmetic  0.9 us (2%)
  between operations  0.9 us (2%)
  local copies, waits for them, and re-layouts  0.73 us (1%)
    all_to_all x1, waiting for transfers between devices, per_device(): lax.all_to_all(outbound.reshape(peers, per_peer, LANES), axes, split_axis...  10.3 us
    all_to_all x1, waiting for transfers between devices, per_device(): lax.all_to_all(picked.reshape(peers, per_peer, LANES), axes, split_axis=0...  8.16 us
    all_to_all x1, starting transfers between devices, per_device(): lax.all_to_all(picked.reshape(peers, per_peer, LANES), axes, split_axis=0...  7.3 us
    pallas_call x1, Pallas kernels, solve_block(): pl.pallas_call(functools.partial(solve_kernel, peers=peers, slot_depth=sl...  6.77 us
    pallas_call x1, Pallas kernels, gather_shell(): pl.pallas_call(functools.partial(gather_kernel, peers=peers, slot_depth=s...  4.89 us
    pallas_call x1, Pallas kernels, scatter_forces(): pl.pallas_call(functools.partial(scatter_kernel, peers=peers, slot_depth=...  4.42 us
    pallas_call x1, Pallas kernels, prepare(): pl.pallas_call(functools.partial(prepare_kernel, plies=plies, side=side),...  4.1 us
    all_to_all x1, starting transfers between devices, per_device(): lax.all_to_all(outbound.reshape(peers, per_peer, LANES), axes, split_axis...  2.79 us
  transfers between devices with their start and end apart: 2, of which 2 were waited for; matrix products, arithmetic and copies ran while one was open for 3% of the time, Pallas kernels for 13%

profile of v5, /device:TPU:0, one launch (start us, length us, event | category | flops | bytes accessed | tf_op | source)
XLA Modules:
  0.0 53.9 jit_solution(12665371144994265425)
XLA Ops:
  0.6 0.0 copy-start.1
  0.6 0.0 copy-start.2
  0.7 4.9 %gather_shell.1 = f32[768,128]{1,0:T(8,128)} custom-call(s32[32,32]{1,0:T(8,128)} %bitcast.21, f32[96,8192]{1,0:T(8,128)} %bitcast.17), custom_call_target="tpu_custom_call" | custom-call | tf_op jit(solution)/shard_map/gather_shell/pallas_call | solution.py:130
  5.5 7.3 %all-to-all-start = ((f32[32,24,128]{2,1,0:T(8,128)}), f32[32,24,128]{2,1,0:T(8,128)S(1)}, u32[]{:S(2)}, u32[]{:S(2)}) async-start(f32[32,24,128]{2,1,0:T(8,128)} %bitcast.19), calls=%async_computation | async-start | bytes 786432 | tf_op jit(solution)/shard_map/all_to_all | solution.py:663
  12.9 0.0 copy-done.1
  12.9 0.1 eq.15
  12.9 0.3 convert_reduce_fusion
  13.2 0.1 reshape.46
  13.3 0.1 copy.20
  13.4 0.1 reshape.47.slot_row_ref
  13.5 0.0 copy-done.2
  13.5 0.6 %cosine_multiply_fusion.cosine_ref = f32[8,48]{1,0:T(8,128)} fusion(s32[8,48]{1,0:T(8,128)S(1)} %copy-done.2), kind=kLoop, calls=%fused_computation.5 | loop fusion | flops 1152 | bytes 3072 | tf_op jit(solution)/shard_map/integer_pow | solution.py:365
  14.1 4.1 %prepare.1.planes_hbm = f32[8,17,8,768]{3,2,1,0:T(8,128)} custom-call(s32[8]{0:T(128)} %active_ref.1, bf16[2,8,16,768]{3,2,1,0:T(8,128)(2,1)} %source_ref.1, bf16[8,16,768]{2,1,0:T(8,128)(2,1)} %knock_ref.1, f32[8,48]{1,0:T(8,128)} %cosine_multiply_fusion.cosine_ref), custom_call_target="tpu_custom_call" | custom-call | flops 40000000 | bytes 12000000 | tf_op jit(solution)/shard_map/prepare/pallas_call | solution.py:368
  18.2 0.0 copy-start
  18.2 8.2 %all-to-all-done = f32[32,24,128]{2,1,0:T(8,128)S(1)} async-done(((f32[32,24,128]{2,1,0:T(8,128)}), f32[32,24,128]{2,1,0:T(8,128)S(1)}, u32[]{:S(2)}, u32[]{:S(2)}) %all-to-all-start) | async-done | bytes 393248 | tf_op jit(solution)/shard_map/all_to_all | solution.py:663
  26.4 6.8 %solve_block.1 = (f32[2,16,8,768]{3,2,1,0:T(8,128)S(1)}, f32[768,128]{1,0:T(8,128)}) custom-call(f32[768,128]{1,0:T(8,128)S(1)} %bitcast.12, f32[8,17,8,768]{3,2,1,0:T(8,128)} %prepare.1.planes_hbm, s32[8,64]{1,0:T(8,128)S(1)} %multiply_add_fusion.slot_ref, s32[1,512]{1,0:T(1,128)S(1)} %reshape.47.slot_row_ref), custom_call_target="tpu_custom_call" | custom-call | tf_op jit(solution)/shard_map/solve_block/pallas_call | solution.py:583
  33.2 2.8 %all-to-all-start.1 = ((f32[32,24,128]{2,1,0:T(8,128)}), f32[32,24,128]{2,1,0:T(8,128)S(1)}, u32[]{:S(2)}, u32[]{:S(2)}) async-start(f32[32,24,128]{2,1,0:T(8,128)} %bitcast.8), calls=%async_computation.1 | async-start | bytes 786432 | tf_op jit(solution)/shard_map/all_to_all | solution.py:676
  36.0 0.0 copy-done
  36.0 0.1 copy.18
  36.1 0.1 copy.22
  36.1 0.1 reshape.49.node_row_ref
  36.2 0.1 copy.21
  36.3 0.1 add.14.row_ref
  36.4 0.4 pair_slots.1.same_ref
  36.8 2.3 %finish.1 = f32[256,768]{1,0:T(8,128)} custom-call(f32[2,16,8,768]{3,2,1,0:T(8,128)S(1)} %get-tuple-element.7.total_ref), custom_call_target="tpu_custom_call" | custom-call | flops 10000000 | bytes 8000000 | tf_op jit(solution)/shard_map/finish/pallas_call | solution.py:637
  39.1 10.3 %all-to-all-done.1 = f32[32,24,128]{2,1,0:T(8,128)S(1)} async-done(((f32[32,24,128]{2,1,0:T(8,128)}), f32[32,24,128]{2,1,0:T(8,128)S(1)}, u32[]{:S(2)}, u32[]{:S(2)}) %all-to-all-start.1) | async-done | bytes 393248 | tf_op jit(solution)/shard_map/all_to_all | solution.py:676
  49.3 4.4 %scatter_forces.1 = f32[96,8192]{1,0:T(8,128)} custom-call(s32[1024]{0:T(1024)S(1)} %add.14.row_ref, bf16[1024,1024]{1,0:T(8,128)(2,1)S(1)} %pair_slots.1.same_ref, f32[768,128]{1,0:T(8,128)S(1)} %bitcast.11), custom_call_target="tpu_custom_call" | custom-call | tf_op jit(solution)/shard_map/scatter_forces/pallas_call | solution.py:214
  (2 shorter events, 0.0 us)
Async XLA Ops:
  0.6 12.2 %copy-start.1 = (s32[8,64]{1,0:T(8,128)S(1)}, s32[8,64]{1,0:T(8,128)}, u32[]{:S(2)}) copy-start(s32[8,64]{1,0:T(8,128)} %param.12) | copy-start | bytes 6148
  0.6 12.8 %copy-start.2 = (s32[8,48]{1,0:T(8,128)S(1)}, s32[8,48]{1,0:T(8,128)}, u32[]{:S(2)}) copy-start(s32[8,48]{1,0:T(8,128)} %param.10) | copy-start | bytes 4612
  5.5 20.9 %all-to-all-start = ((f32[32,24,128]{2,1,0:T(8,128)}), f32[32,24,128]{2,1,0:T(8,128)S(1)}, u32[]{:S(2)}, u32[]{:S(2)}) async-start(f32[32,24,128]{2,1,0:T(8,128)} %bitcast.19), calls=%async_computation | async-start | bytes 786432 | tf_op jit(solution)/shard_map/all_to_all | solution.py:663
  18.2 17.8 %copy-start = (s32[1,32,32]{2,1,0:T(8,128)S(1)}, s32[1,32,32]{2,1,0:T(8,128)}, u32[]{:S(2)}) copy-start(s32[1,32,32]{2,1,0:T(8,128)} %param.13) | copy-start | bytes 12292
  33.2 16.2 %all-to-all-start.1 = ((f32[32,24,128]{2,1,0:T(8,128)}), f32[32,24,128]{2,1,0:T(8,128)S(1)}, u32[]{:S(2)}, u32[]{:S(2)}) async-start(f32[32,24,128]{2,1,0:T(8,128)} %bitcast.8), calls=%async_computation.1 | async-start | bytes 786432 | tf_op jit(solution)/shard_map/all_to_all | solution.py:676

commit v6 on v5

--- a/solution.py
+++ b/solution.py
@@ -246,7 +246,7 @@
 
 
 def prepare_kernel(
-    active_ref, source_ref, knock_ref, cosine_ref, planes_hbm,
+    active_ref, source_ref, knock_ref, cosine_ref, slot_ref, planes_hbm, hit,
     planes, src, knock, ply_ref, sems, *, plies, side,
 ):
     cases, subs, cells_x, width = source_ref.shape
@@ -256,6 +256,14 @@
     first_y = y_place == 0
     last_y = y_place == side - 1
     cut = [slice(t * LANES, (t + 1) * LANES) for t in range(tiles)]
+
+    slot_lane = lax.broadcasted_iota(jnp.int32, (subs, hit.shape[1]), 1)
+    for pair in range(2 * side):
+        both = [
+            jnp.where(slot_lane == slot_ref[:, q : q + 1], 1.0, 0.0)
+            for q in (2 * pair, 2 * pair + 1)
+        ]
+        hit[pair * 2 * subs : (pair + 1) * 2 * subs, :] = jnp.concatenate(both, axis=0).astype(BF16)
 
     ply = lax.broadcasted_iota(jnp.int32, (subs, plies), 1)
     sub = lax.broadcasted_iota(jnp.int32, (subs, plies), 0)
@@ -293,7 +301,7 @@
     def plane(ref, x, base=0):
         return [ref[t, pl.ds(base + x, subs, stride=cells_x), :] for t in range(tiles)]
 
-    face_x, face_y, face_p, diag, inverse, along_y = (planes.at[k] for k in range(6))
+    face_x, face_y, face_p, inverse, along_y = (planes.at[k] for k in range(5))
     face_x[0] = jnp.zeros((subs, width), F32)
     face_x[cells_x] = jnp.zeros((subs, width), F32)
 
@@ -332,18 +340,17 @@
             )
             face_y[x, :, cut[t]] = fy
             face_p[x, :, cut[t]] = fp[t]
-            diag[x, :, cut[t]] = whole
             inverse[x, :, cut[t]] = 1.0 / whole
             along_y[x, :, cut[t]] = ay[t]
             for c in range(cases):
                 value = src[t, pl.ds(c * subs * cells_x + x, subs, stride=cells_x), :]
-                planes[6 + c, x, :, cut[t]] = ply_ref[2, :, cut[t]] * value
+                planes[5 + c, x, :, cut[t]] = ply_ref[2, :, cut[t]] * value
         return carry
 
     for e, x in enumerate((0, cells_x - 1)):
         k = plane(knock, x)
         for t in range(tiles):
-            planes[1 + e, cells_x, :, cut[t]] = k[t] * ply_ref[0, :, cut[t]]
+            planes[3 + e, cells_x, :, cut[t]] = k[t] * ply_ref[0, :, cut[t]]
     bands = sems.shape[0]
     band = cells_x // bands
     copies = []
@@ -358,18 +365,21 @@
         copy.wait()
 
 
-def prepare(source, knockdown, orient, active):
+def prepare(source, knockdown, orient, active, slot_index, slots):
     cases, subs, cells_x, width = source.shape
     plies = orient.shape[1]
     side = width // plies
     cosine = jnp.cos(orient.astype(F32) * (math.pi / 6.0)) ** 2
-    planes = (6 + cases, cells_x + 1, subs, width)
+    planes = (5 + cases, cells_x + 1, subs, width)
     vm = pl.BlockSpec(memory_space=pltpu.VMEM)
     return pl.pallas_call(
         functools.partial(prepare_kernel, plies=plies, side=side),
-        out_shape=jax.ShapeDtypeStruct(planes, F32),
-        in_specs=[pl.BlockSpec(memory_space=pltpu.SMEM)] + [vm] * 3,
-        out_specs=pl.BlockSpec(memory_space=pltpu.HBM),
+        out_shape=(
+            jax.ShapeDtypeStruct(planes, F32),
+            jax.ShapeDtypeStruct((slot_index.size, slots), BF16),
+        ),
+        in_specs=[pl.BlockSpec(memory_space=pltpu.SMEM)] + [vm] * 4,
+        out_specs=(pl.BlockSpec(memory_space=pltpu.HBM), vm),
         scratch_shapes=[
             pltpu.VMEM(planes, F32),
             pltpu.VMEM((width // LANES, cases * subs * cells_x, LANES), F32),
@@ -377,28 +387,28 @@
             pltpu.VMEM((4, subs, width), F32),
             pltpu.SemaphoreType.DMA((4,)),
         ],
-        compiler_params=pltpu.CompilerParams(vmem_limit_bytes=58 << 20),
+        compiler_params=pltpu.CompilerParams(vmem_limit_bytes=52 << 20),
         cost_estimate=pl.CostEstimate(
             flops=40_000_000, bytes_accessed=12_000_000, transcendentals=0
         ),
         name="prepare",
-    )(active, source, knockdown, cosine)
+    )(active, source, knockdown, cosine, slot_index)
 
 
 def solve_kernel(
-    packed_ref, planes_hbm, slot_ref, slot_row_ref, total, out_ref,
-    planes, slots, hit, bound, work, resid, side_y, side_x, tall, sems,
+    packed_ref, planes_hbm, hit_ref, slot_row_ref, total, out_ref,
+    planes, slots, bound, work, resid, side_y, side_x, tall, sems,
     *, peers, slot_depth, side,
 ):
     cases, cells_x, subs, width = total.shape
-    parts = [slice(4, 6 + cases), slice(1, 3), slice(0, 1), slice(3, 4)]
+    parts = [slice(3, 5 + cases), slice(0, 3)]
     copies = [
         pltpu.make_async_copy(planes_hbm.at[part], planes.at[part], sems.at[k])
         for k, part in enumerate(parts)
     ]
     for copy in copies:
         copy.start()
-    face_x, face_y, face_p, diag, inverse, along_y = (planes.at[k] for k in range(6))
+    face_x, face_y, face_p, inverse, along_y = (planes.at[k] for k in range(5))
     tiles = width // LANES
     lane = lax.broadcasted_iota(jnp.int32, (subs, LANES), 1)
     y_place = lane % side
@@ -412,14 +422,7 @@
 
     unpack_slots(packed_ref, slots, peers, slot_depth)
     pieces = jnp.concatenate(split_two(slots[...]), axis=1)
-    slot_lane = lax.broadcasted_iota(jnp.int32, (subs, peers * slot_depth), 1)
-    for pair in range(2 * side):
-        both = [
-            jnp.where(slot_lane == slot_ref[:, q : q + 1], 1.0, 0.0)
-            for q in (2 * pair, 2 * pair + 1)
-        ]
-        hit[pair * 2 * subs : (pair + 1) * 2 * subs, :] = jnp.concatenate(both, axis=0).astype(BF16)
-    found = jnp.dot(hit[...], pieces, preferred_element_type=F32)
+    found = jnp.dot(hit_ref[...], pieces, preferred_element_type=F32)
     rows = side * subs
     lower = lax.broadcasted_iota(jnp.int32, (4 * rows, LANES), 1) < HALF
     high, low = found[:, :LANES], found[:, LANES:]
@@ -449,7 +452,6 @@
                     gathered = jnp.where(y_place == q, part, gathered)
                 side_x[c, e, :, cut[t]] = gathered
     copies[0].wait()
-    copies[1].wait()
 
     def residual(x, carry):
         at_first = jnp.where(x == 0, 1.0, 0.0)
@@ -458,18 +460,17 @@
         for c in range(cases):
             for t in range(tiles):
                 value = (
-                    planes[6 + c, x, :, cut[t]]
+                    planes[5 + c, x, :, cut[t]]
                     + along_y[x, :, cut[t]] * side_y[pl.ds(c * rows + row, subs), cut[t]]
-                    + at_first * (planes[1, cells_x, :, cut[t]] * side_x[c, 0, :, cut[t]])
-                    + at_final * (planes[2, cells_x, :, cut[t]] * side_x[c, 1, :, cut[t]])
+                    + at_first * (planes[3, cells_x, :, cut[t]] * side_x[c, 0, :, cut[t]])
+                    + at_final * (planes[4, cells_x, :, cut[t]] * side_x[c, 1, :, cut[t]])
                 )
                 resid[c, x, :, cut[t]] = value
                 work[0, c, x + 1, :, cut[t]] = (value * inverse[x, :, cut[t]]) * (1.0 / CHEB_CENTER)
         return carry
 
     lax.fori_loop(0, cells_x, residual, 0, unroll=4)
-    copies[2].wait()
-    copies[3].wait()
+    copies[1].wait()
 
     def operate(x, c, old):
         w = [work[old, c, x + 1, :, cut[t]] for t in range(tiles)]
@@ -486,7 +487,7 @@
                 + fy * pltpu.roll(w[t], LANES - 1, 1)
                 + (below[t] + fp[t] * above[t])
             )
-            out.append(diag[x, :, cut[t]] * w[t] - beside)
+            out.append(beside)
         return w, out
 
     sigma = CHEB_CENTER / CHEB_HALF
@@ -500,16 +501,17 @@
 
         def second(x, carry, sweep=sweep, final=final):
             for c in range(cases):
-                w, moved = operate(x, c, 0)
+                w, beside = operate(x, c, 0)
                 for t in range(tiles):
-                    r = resid[c, x, :, cut[t]] - moved[t]
+                    before = resid[c, x, :, cut[t]]
+                    r = (1.0 - 1.0 / CHEB_CENTER) * before + beside[t]
                     later = keep * w[t] + gain * (r * inverse[x, :, cut[t]])
                     sums = w[t] + later
                     if sweep:
                         sums = total[c, x, :, cut[t]] + sums
                     total[c, x, :, cut[t]] = sums
                     if not final:
-                        resid[c, x, :, cut[t]] = r
+                        resid[c, x, :, cut[t]] = (1.0 - gain) * r - (keep / CHEB_CENTER) * before
                         work[1, c, x + 1, :, cut[t]] = later
                     else:
                         row = pl.multiple_of(x * subs, subs)
@@ -524,9 +526,9 @@
 
         def first(x, carry):
             for c in range(cases):
-                _, moved = operate(x, c, 1)
+                _, beside = operate(x, c, 1)
                 for t in range(tiles):
-                    r = resid[c, x, :, cut[t]] - moved[t]
+                    r = resid[c, x, :, cut[t]] + beside[t]
                     resid[c, x, :, cut[t]] = r
                     work[0, c, x + 1, :, cut[t]] = (r * inverse[x, :, cut[t]]) * (1.0 / CHEB_CENTER)
             return carry
@@ -536,7 +538,7 @@
     y_wide = lax.broadcasted_iota(jnp.int32, (subs, width), 1) % side
     for c in range(cases):
         for e, x in enumerate((0, cells_x - 1)):
-            at_ply = planes[1 + e, cells_x] * (side_x[c, e] - total[c, x])
+            at_ply = planes[3 + e, cells_x] * (side_x[c, e] - total[c, x])
             for k, piece in enumerate(split_two(at_ply)):
                 wide = piece.astype(F32)
                 at = ((2 * c + e) * 2 + k) * rows
@@ -573,7 +575,7 @@
     pack_slots(slots, out_ref, peers, slot_depth)
 
 
-def solve_block(packed, ready, slot_index, source, peers, slot_depth, side):
+def solve_block(packed, ready, hit, slot_index, source, peers, slot_depth, side):
     cases, subs, cells_x, width = source.shape
     points = slot_index.shape[1]
     vm = pl.BlockSpec(memory_space=pltpu.VMEM)
@@ -591,18 +593,17 @@
         scratch_shapes=[
             pltpu.VMEM(ready.shape, F32),
             pltpu.VMEM((peers * slot_depth, LANES), F32),
-            pltpu.VMEM((points * subs, peers * slot_depth), BF16),
             pltpu.VMEM((cases, 4 * side * subs, LANES), BF16),
             pltpu.VMEM((2, cases, cells_x + 2, subs, width), F32),
             pltpu.VMEM((cases,) + planes, F32),
             pltpu.VMEM((cases * side * subs, width), F32),
             pltpu.VMEM((cases, 2, subs, width), F32),
             pltpu.VMEM((4 * cases * side * subs, width), BF16),
-            pltpu.SemaphoreType.DMA((4,)),
+            pltpu.SemaphoreType.DMA((2,)),
         ],
         compiler_params=pltpu.CompilerParams(vmem_limit_bytes=51 << 20),
         name="solve_block",
-    )(packed, ready, slot_index, slot_index.T.reshape(1, points * subs))
+    )(packed, ready, hit, slot_index.T.reshape(1, points * subs))
 
 
 def finish_kernel(total_ref, adjoint_ref, turned, *, side):
@@ -669,9 +670,11 @@
     earlier = (owners[:, None] == owners[None, :]) & (place[None, :] < place[:, None])
     rank = jnp.sum(earlier.astype(jnp.int32), axis=1).reshape(point_owner.shape)
     slot_index = point_owner * slot_depth + rank
-    ready = prepare(source, knockdown, orient, active)
+    ready, hit = prepare(
+        source, knockdown, orient, active, slot_index, peers * slot_depth
+    )
     planes, outbound = solve_block(
-        arrived.reshape(peers * per_peer, LANES), ready, slot_index, source, peers, slot_depth, side
+        arrived.reshape(peers * per_peer, LANES), ready, hit, slot_index, source, peers, slot_depth, side
     )
     returned = lax.all_to_all(
         outbound.reshape(peers, per_peer, LANES), axes, split_axis=0, concat_axis=0, tiled=True

time: 54.3 us -> 54.3 us (level)
  waiting for transfers between devices: 18.4 us -> 19.6 us
  Pallas kernels: 22.9 us -> 22.1 us
  other arithmetic: 0.9 us -> 0.31 us
    all_to_all x1, waiting for transfers between devices: 8.16 us -> 9.37 us  [per_device(): lax.all_to_all(picked.reshape(peers, per_peer, LANES), axes, split_axis=0...]
    pallas_call x1, Pallas kernels: 4.1 us -> 3.48 us  [prepare(): pl.pallas_call(functools.partial(prepare_kernel, plies=plies, side=side),...]
    integer_pow x1, other arithmetic: 0.64 us -> 0.04 us  [prepare(): cosine = jnp.cos(orient.astype(F32) * (math.pi / 6.0)) ** 2]
  transfers between devices with their start and end apart: 2 -> 2, of which waited for: 2 -> 2; matrix products, arithmetic and copies ran while one was open for 3% -> 2% of each run, Pallas kernels for 13% -> 11%
where the time goes in v6:
time: 54.3 us; the launch traced here: 53.8 us
  Pallas kernels  22.1 us (41%)
  waiting for transfers between devices  19.6 us (36%)
  starting transfers between devices  10.1 us (19%)
  between operations  0.94 us (2%)
  local copies, waits for them, and re-layouts  0.74 us (1%)
    all_to_all x1, waiting for transfers between devices, per_device(): lax.all_to_all(outbound.reshape(peers, per_peer, LANES), axes, split_axis...  10.3 us
    all_to_all x1, waiting for transfers between devices, per_device(): lax.all_to_all(picked.reshape(peers, per_peer, LANES), axes, split_axis=0...  9.37 us
    all_to_all x1, starting transfers between devices, per_device(): lax.all_to_all(picked.reshape(peers, per_peer, LANES), axes, split_axis=0...  7.31 us
    pallas_call x1, Pallas kernels, solve_block(): pl.pallas_call(functools.partial(solve_kernel, peers=peers, slot_depth=sl...  6.64 us
    pallas_call x1, Pallas kernels, gather_shell(): pl.pallas_call(functools.partial(gather_kernel, peers=peers, slot_depth=s...  4.88 us
    pallas_call x1, Pallas kernels, scatter_forces(): pl.pallas_call(functools.partial(scatter_kernel, peers=peers, slot_depth=...  4.42 us
    pallas_call x1, Pallas kernels, prepare(): pl.pallas_call(functools.partial(prepare_kernel, plies=plies, side=side),...  3.48 us
    all_to_all x1, starting transfers between devices, per_device(): lax.all_to_all(outbound.reshape(peers, per_peer, LANES), axes, split_axis...  2.79 us
  transfers between devices with their start and end apart: 2, of which 2 were waited for; matrix products, arithmetic and copies ran while one was open for 2% of the time, Pallas kernels for 11%

profile of v6, /device:TPU:0, one launch (start us, length us, event | category | flops | bytes accessed | tf_op | source)
XLA Modules:
  0.0 53.8 jit_solution(15749227598965193914)
XLA Ops:
  0.6 0.0 copy-start.4
  0.6 0.0 copy-start.5
  0.7 0.0 copy-start.2
  0.7 0.0 copy-start.1
  0.7 0.0 copy-start
  0.7 4.9 %gather_shell.1 = f32[768,128]{1,0:T(8,128)} custom-call(s32[32,32]{1,0:T(8,128)} %bitcast.21, f32[96,8192]{1,0:T(8,128)} %bitcast.17), custom_call_target="tpu_custom_call" | custom-call | tf_op jit(solution)/shard_map/gather_shell/pallas_call | solution.py:130
  5.6 0.0 copy-start.3
  5.6 7.3 %all-to-all-start = ((f32[32,24,128]{2,1,0:T(8,128)}), f32[32,24,128]{2,1,0:T(8,128)S(1)}, u32[]{:S(2)}, u32[]{:S(2)}) async-start(f32[32,24,128]{2,1,0:T(8,128)} %bitcast.19), calls=%async_computation | async-start | bytes 786432 | tf_op jit(solution)/shard_map/all_to_all | solution.py:664
  12.9 0.0 copy-done.4
  12.9 0.1 eq.15
  13.0 0.3 convert_reduce_fusion
  13.2 0.1 reshape.46
  13.3 0.1 copy.20
  13.4 0.1 reshape.47.slot_row_ref
  13.5 0.0 copy-done.5
  13.6 0.0 copy-done.2
  13.6 0.0 copy-done.1
  13.6 0.0 copy-done
  13.6 3.5 %prepare.1 = (f32[7,17,8,768]{3,2,1,0:T(8,128)}, bf16[512,1024]{1,0:T(8,128)(2,1)S(1)}) custom-call(s32[8]{0:T(128)S(1)} %copy-done.2, bf16[2,8,16,768]{3,2,1,0:T(8,128)(2,1)S(1)} %copy-done, bf16[8,16,768]{2,1,0:T(8,128)(2,1)S(1)} %copy-done.1, f32[8,48]{1,0:T(8,128)S(1)} %cosine_multiply_fusion.cosine_ref, s32[8,64]{1,0:T(8,128)S(1)} %multiply_add_fusion.slot_ref), custom_call_target="tpu_custom_call" | custom-call | flops 40000000 | bytes 12000000 | tf_op jit(solution)/shard_map/prepare/pallas_call | solution.py:375
  17.1 9.4 %all-to-all-done = f32[32,24,128]{2,1,0:T(8,128)S(1)} async-done(((f32[32,24,128]{2,1,0:T(8,128)}), f32[32,24,128]{2,1,0:T(8,128)S(1)}, u32[]{:S(2)}, u32[]{:S(2)}) %all-to-all-start) | async-done | bytes 393248 | tf_op jit(solution)/shard_map/all_to_all | solution.py:664
  26.4 6.6 %solve_block.1 = (f32[2,16,8,768]{3,2,1,0:T(8,128)S(1)}, f32[768,128]{1,0:T(8,128)}) custom-call(f32[768,128]{1,0:T(8,128)S(1)} %bitcast.12, f32[7,17,8,768]{3,2,1,0:T(8,128)} %get-tuple-element.8.planes_hbm, bf16[512,1024]{1,0:T(8,128)(2,1)S(1)} %get-tuple-element.9.hit_ref, s32[1,512]{1,0:T(1,128)S(1)} %reshape.47.slot_row_ref), custom_call_target="tpu_custom_call" | custom-call | tf_op jit(solution)/shard_map/solve_block/pallas_call | solution.py:585
  33.1 2.8 %all-to-all-start.1 = ((f32[32,24,128]{2,1,0:T(8,128)}), f32[32,24,128]{2,1,0:T(8,128)S(1)}, u32[]{:S(2)}, u32[]{:S(2)}) async-start(f32[32,24,128]{2,1,0:T(8,128)} %bitcast.8), calls=%async_computation.1 | async-start | bytes 786432 | tf_op jit(solution)/shard_map/all_to_all | solution.py:679
  35.9 0.0 copy-done.3
  35.9 0.1 copy.18
  36.0 0.1 copy.22
  36.0 0.1 reshape.49.node_row_ref
  36.1 0.1 copy.21
  36.2 0.1 add.14.row_ref
  36.3 0.4 pair_slots.1.same_ref
  36.7 2.3 %finish.1 = f32[256,768]{1,0:T(8,128)} custom-call(f32[2,16,8,768]{3,2,1,0:T(8,128)S(1)} %get-tuple-element.11.total_ref), custom_call_target="tpu_custom_call" | custom-call | flops 10000000 | bytes 8000000 | tf_op jit(solution)/shard_map/finish/pallas_call | solution.py:638
  39.0 10.3 %all-to-all-done.1 = f32[32,24,128]{2,1,0:T(8,128)S(1)} async-done(((f32[32,24,128]{2,1,0:T(8,128)}), f32[32,24,128]{2,1,0:T(8,128)S(1)}, u32[]{:S(2)}, u32[]{:S(2)}) %all-to-all-start.1) | async-done | bytes 393248 | tf_op jit(solution)/shard_map/all_to_all | solution.py:679
  49.3 4.4 %scatter_forces.1 = f32[96,8192]{1,0:T(8,128)} custom-call(s32[1024]{0:T(1024)S(1)} %add.14.row_ref, bf16[1024,1024]{1,0:T(8,128)(2,1)S(1)} %pair_slots.1.same_ref, f32[768,128]{1,0:T(8,128)S(1)} %bitcast.11), custom_call_target="tpu_custom_call" | custom-call | tf_op jit(solution)/shard_map/scatter_forces/pallas_call | solution.py:214
  (3 shorter events, 0.1 us)
Async XLA Ops:
  0.6 12.3 %copy-start.4 = (s32[8,64]{1,0:T(8,128)S(1)}, s32[8,64]{1,0:T(8,128)}, u32[]{:S(2)}) copy-start(s32[8,64]{1,0:T(8,128)} %param.12) | copy-start | bytes 6148
  0.6 12.9 %copy-start.5 = (s32[8,48]{1,0:T(8,128)S(1)}, s32[8,48]{1,0:T(8,128)}, u32[]{:S(2)}) copy-start(s32[8,48]{1,0:T(8,128)} %param.10) | copy-start | bytes 4612
  0.7 12.9 %copy-start.2 = (s32[8]{0:T(128)S(1)}, s32[8]{0:T(128)}, u32[]{:S(2)}) copy-start(s32[8]{0:T(128)} %active_ref.1) | copy-start | bytes 100
  0.7 12.9 %copy-start.1 = (bf16[8,16,768]{2,1,0:T(8,128)(2,1)S(1)}, bf16[8,16,768]{2,1,0:T(8,128)(2,1)}, u32[]{:S(2)}) copy-start(bf16[8,16,768]{2,1,0:T(8,128)(2,1)} %knock_ref.1) | copy-start | bytes 589828
  0.7 12.9 %copy-start = (bf16[2,8,16,768]{3,2,1,0:T(8,128)(2,1)S(1)}, bf16[2,8,16,768]{3,2,1,0:T(8,128)(2,1)}, u32[]{:S(2)}) copy-start(bf16[2,8,16,768]{3,2,1,0:T(8,128)(2,1)} %source_ref.1) | copy-start | bytes 1179652
  5.6 30.3 %copy-start.3 = (s32[1,32,32]{2,1,0:T(8,128)S(1)}, s32[1,32,32]{2,1,0:T(8,128)}, u32[]{:S(2)}) copy-start(s32[1,32,32]{2,1,0:T(8,128)} %param.13) | copy-start | bytes 12292
  5.6 20.9 %all-to-all-start = ((f32[32,24,128]{2,1,0:T(8,128)}), f32[32,24,128]{2,1,0:T(8,128)S(1)}, u32[]{:S(2)}, u32[]{:S(2)}) async-start(f32[32,24,128]{2,1,0:T(8,128)} %bitcast.19), calls=%async_computation | async-start | bytes 786432 | tf_op jit(solution)/shard_map/all_to_all | solution.py:664
  33.1 16.2 %all-to-all-start.1 = ((f32[32,24,128]{2,1,0:T(8,128)}), f32[32,24,128]{2,1,0:T(8,128)S(1)}, u32[]{:S(2)}, u32[]{:S(2)}) async-start(f32[32,24,128]{2,1,0:T(8,128)} %bitcast.8), calls=%async_computation.1 | async-start | bytes 786432 | tf_op jit(solution)/shard_map/all_to_all | solution.py:679
